TPU v7x, 32 devices: a whole 2x2x4 slice. The times are simulated.
32 devices in a mesh: batch: 4 (over x, core), blk: 8 (over z, y).
Axes of the slice: x: 2, y: 2, z: 4, core: 2. Of those that a mesh axis runs over, the one named last changes fastest.
Arguments:
- inputs: bfloat16 [8, 1024, 1024], P('batch', 'blk'), may hold values from -6 to 6
- time_embed: bfloat16 [8, 1024], P('batch'), may hold values from -6 to 6
- lengths: int32 [8], P('batch'), may hold values from 64 to 1024, as said below
- cotangent: bfloat16 [8, 1024, 1024], P('batch', 'blk'), may hold values from -6 to 6
- w_mod: bfloat16 [1024, 6144], replicated, may hold values from -0.1875 to 0.1875
- b_mod: bfloat16 [6144], replicated, may hold values from -3 to 3
- w_qkv: bfloat16 [1024, 3072], replicated, may hold values from -0.1875 to 0.1875
- b_qkv: bfloat16 [3072], replicated, may hold values from -2 to 2
- w_out: bfloat16 [1024, 1024], replicated, may hold values from -2 to 2
- b_out: bfloat16 [1024], replicated, may hold values from -2 to 2
- w_up: bfloat16 [1024, 2048], replicated, may hold values from -0.1875 to 0.1875
- b_up: bfloat16 [2048], replicated, may hold values from -3 to 3
- w_down: bfloat16 [2048, 1024], replicated, may hold values from -0.125 to 0.125
- b_down: bfloat16 [1024], replicated, may hold values from -2 to 2
Outputs:
- output: float32 [8, 1024, 1024], P('batch', 'blk')
- grad_inputs: float32 [8, 1024, 1024], P('batch', 'blk')
- grad_time: float32 [8, 1024], P('batch')
- grad_w_mod: float32 [1024, 6144], P('blk')
- grad_b_mod: float32 [6144], P('blk')
- grad_w_qkv: float32 [1024, 3072], P('blk')
- grad_b_qkv: float32 [3072], P('blk')
- grad_w_out: float32 [1024, 1024], P('blk')
- grad_b_out: float32 [1024], P('blk')
- grad_w_up: float32 [1024, 2048], P('blk')
- grad_b_up: float32 [2048], P('blk')
- grad_w_down: float32 [2048, 1024], P('blk')
- grad_b_down: float32 [1024], P('blk')
Inputs may be any that keep to these rules, and one draw needn't show every extreme that they name: `lengths`: lengths are counted in mel frames, from 64 to 1024. Among the 2 utterances of each index of batch, one drawn from the seed has exactly 1024 frames and another exactly 64.
All inputs are finite; a program needn't handle non-finite values.
Results may differ from a plain program's by a relative error of at most 0.017.
Values may be sent and summed in bfloat16 or wider, within the bound.
A program may use at most 192 MiB of HBM per device.

v0:
```python
from functools import partial

import jax
import jax.numpy as jnp
from jax import lax
from jax.sharding import PartitionSpec as P

HEADS = 16


EPS = 1e-06
NEG = -1e30
HIGH = lax.Precision.HIGHEST


def from_behind(block, axis, distance):
    devices = range(lax.axis_size(axis))
    route = [((i - distance) % len(devices), i) for i in devices]
    return lax.ppermute(block, axis, route)


def normalize(rows):
    mean = jnp.mean(rows, axis=-1, keepdims=True)
    centered = rows - mean
    inverse = lax.rsqrt(jnp.mean(centered * centered, axis=-1, keepdims=True) + EPS)
    return (centered * inverse, inverse)


def norm_back(normed, inverse, grad):
    return inverse * (
        grad
        - jnp.mean(grad, axis=-1, keepdims=True)
        - normed * jnp.mean(grad * normed, axis=-1, keepdims=True)
    )


def angles_for(positions, half):
    freqs = 10000.0 ** (-jnp.arange(half, dtype=jnp.float32) / half)
    angle = positions.astype(jnp.float32)[:, None] * freqs[None, :]
    return (jnp.cos(angle)[:, None, :], jnp.sin(angle)[:, None, :])


def turn(parts, cosines, sines, sign):
    half = parts.shape[-1] // 2
    first = parts[..., :half]
    second = parts[..., half:]
    return jnp.concatenate(
        [first * cosines - sign * (second * sines), second * cosines + sign * (first * sines)],
        axis=-1,
    )


def scores_of(query_heads, key_heads, valid):
    scale = query_heads.shape[-1] ** (-0.5)
    raw = (
        jnp.einsum("sqhd,skhd->shqk", query_heads, key_heads, preferred_element_type=jnp.float32)
        * scale
    )
    return jnp.where(valid[:, None, None, :], raw, NEG)


def row_product(left, right):
    return lax.dot_general(
        left, right, (((1,), (1,)), ((), ())), preferred_element_type=jnp.float32
    )


def on_device(
    inputs,
    time_embed,
    lengths,
    cotangent,
    w_mod,
    b_mod,
    w_qkv,
    b_qkv,
    w_out,
    b_out,
    w_up,
    b_up,
    w_down,
    b_down,
):
    seq_count, frame_count, width = inputs.shape
    head_count = HEADS
    head_dim = width // head_count
    cycle_size = lax.axis_size("blk")
    own_index = lax.axis_index("blk")
    frame_span = jnp.arange(frame_count, dtype=jnp.int32)
    cosines, sines = angles_for(own_index * frame_count + frame_span, head_dim // 2)

    def key_valid(start, count):
        return (start + jnp.arange(count, dtype=jnp.int32))[None, :] < lengths[:, None]

    def split_heads(flat):
        return flat.reshape(seq_count, -1, head_count, head_dim)

    def join_heads(heads):
        return heads.reshape(seq_count, -1, width)

    embed_f32 = time_embed.astype(jnp.float32)
    time_silu, silu_pull = jax.vjp(jax.nn.silu, embed_f32)
    time_act = time_silu.astype(jnp.bfloat16)
    mods = jnp.dot(time_act, w_mod, preferred_element_type=jnp.float32) + b_mod.astype(jnp.float32)
    shift_a, scale_a, gate_a, shift_f, scale_f, gate_f = [
        piece[:, None, :] for piece in jnp.split(mods, 6, axis=-1)
    ]
    residual = inputs.astype(jnp.float32)
    norm_a, inverse_a = normalize(residual)
    hidden_a = (norm_a * (1.0 + scale_a) + shift_a).astype(jnp.bfloat16).reshape(-1, width)
    projected = jnp.dot(hidden_a, w_qkv, preferred_element_type=jnp.float32) + b_qkv.astype(
        jnp.float32
    )
    projected = projected.reshape(seq_count, frame_count, 3, head_count, head_dim)
    queries = turn(projected[:, :, 0], cosines, sines, 1.0).astype(jnp.bfloat16)
    keys = turn(projected[:, :, 1], cosines, sines, 1.0).astype(jnp.bfloat16)
    values = projected[:, :, 2].astype(jnp.bfloat16)

    def absorb(state, key_flat, value_flat, valid):
        running_top, running_total, running_sum = state
        scores = scores_of(queries, split_heads(key_flat), valid)
        new_top = jnp.maximum(running_top, jnp.max(scores, axis=-1))
        factor = jnp.exp(running_top - new_top)
        weights = jnp.exp(scores - new_top[..., None])
        running_total = running_total * factor + jnp.sum(weights, axis=-1)
        running_sum = running_sum * factor[..., None] + jnp.einsum(
            "shqk,skhd->shqd",
            weights.astype(jnp.bfloat16),
            split_heads(value_flat),
            preferred_element_type=jnp.float32,
        )
        return (new_top, running_total, running_sum)

    start_state = (
        jnp.full((seq_count, head_count, frame_count), NEG, jnp.float32),
        jnp.zeros((seq_count, head_count, frame_count), jnp.float32),
        jnp.zeros((seq_count, head_count, frame_count, head_dim), jnp.float32),
    )
    keys_flat = join_heads(keys)
    values_flat = join_heads(values)
    first_state = absorb(
        start_state, keys_flat, values_flat, key_valid(own_index * frame_count, frame_count)
    )

    def forward_turn(step, carry):
        key_flat, value_flat, state = carry
        key_flat, value_flat = from_behind((key_flat, value_flat), "blk", 1)
        owner = (own_index - step) % cycle_size
        return (
            key_flat,
            value_flat,
            absorb(state, key_flat, value_flat, key_valid(owner * frame_count, frame_count)),
        )

    spent_keys, spent_values, final_state = lax.fori_loop(
        1, cycle_size, forward_turn, (keys_flat, values_flat, first_state)
    )
    running_top, running_total, running_sum = final_state
    attn = (running_sum / running_total[..., None]).transpose(0, 2, 1, 3)
    log_total = running_top + jnp.log(running_total)
    attn_low = attn.reshape(-1, width).astype(jnp.bfloat16)
    branch_a = (
        jnp.dot(attn_low, w_out, preferred_element_type=jnp.float32) + b_out.astype(jnp.float32)
    ).reshape(seq_count, frame_count, width)
    mixed = residual + gate_a * branch_a
    norm_f, inverse_f = normalize(mixed)
    hidden_f = (norm_f * (1.0 + scale_f) + shift_f).astype(jnp.bfloat16).reshape(-1, width)
    pre_act = jnp.dot(hidden_f, w_up, preferred_element_type=jnp.float32) + b_up.astype(jnp.float32)
    act_f32, gelu_pull = jax.vjp(partial(jax.nn.gelu, approximate=True), pre_act)
    act_low = act_f32.astype(jnp.bfloat16)
    branch_f = (
        jnp.dot(act_low, w_down, preferred_element_type=jnp.float32) + b_down.astype(jnp.float32)
    ).reshape(seq_count, frame_count, width)
    output = mixed + gate_f * branch_f
    grad_out = cotangent.astype(jnp.float32)
    grad_gate_f = jnp.sum(grad_out * branch_f, axis=1)
    grad_ff = (gate_f * grad_out).astype(jnp.bfloat16).reshape(-1, width)
    grad_w_down = jnp.dot(act_low.T, grad_ff, preferred_element_type=jnp.float32)
    grad_b_down = jnp.sum(grad_ff.astype(jnp.float32), axis=0)
    grad_pre = gelu_pull(row_product(grad_ff, w_down))[0].astype(jnp.bfloat16)
    grad_w_up = jnp.dot(hidden_f.T, grad_pre, preferred_element_type=jnp.float32)
    grad_b_up = jnp.sum(grad_pre.astype(jnp.float32), axis=0)
    grad_hidden_f = row_product(grad_pre, w_up).reshape(seq_count, frame_count, width)
    grad_scale_f = jnp.sum(grad_hidden_f * norm_f, axis=1)
    grad_shift_f = jnp.sum(grad_hidden_f, axis=1)
    grad_mixed = grad_out + norm_back(norm_f, inverse_f, grad_hidden_f * (1.0 + scale_f))
    grad_gate_a = jnp.sum(grad_mixed * branch_a, axis=1)
    grad_branch_a = (gate_a * grad_mixed).astype(jnp.bfloat16).reshape(-1, width)
    grad_w_out = jnp.dot(attn_low.T, grad_branch_a, preferred_element_type=jnp.float32)
    grad_b_out = jnp.sum(grad_branch_a.astype(jnp.float32), axis=0)
    grad_attn = (
        row_product(grad_branch_a, w_out)
        .astype(jnp.bfloat16)
        .reshape(seq_count, frame_count, head_count, head_dim)
    )
    delta = jnp.sum(grad_attn.astype(jnp.float32) * attn, axis=-1).transpose(0, 2, 1)

    def block_grads(query_heads, grad_heads, log_sum, delta_rows, key_heads, value_heads, valid):
        scale = head_dim ** (-0.5)
        scores = scores_of(query_heads, key_heads, valid)
        probs = jnp.exp(scores - log_sum[..., None])
        grad_values = jnp.einsum(
            "shqk,sqhd->skhd",
            probs.astype(jnp.bfloat16),
            grad_heads,
            preferred_element_type=jnp.float32,
        )
        grad_probs = jnp.einsum(
            "sqhd,skhd->shqk", grad_heads, value_heads, preferred_element_type=jnp.float32
        )
        grad_scores = (probs * (grad_probs - delta_rows[..., None])).astype(jnp.bfloat16)
        grad_queries = (
            jnp.einsum(
                "shqk,skhd->sqhd", grad_scores, key_heads, preferred_element_type=jnp.float32
            )
            * scale
        )
        grad_keys = (
            jnp.einsum(
                "shqk,sqhd->skhd", grad_scores, query_heads, preferred_element_type=jnp.float32
            )
            * scale
        )
        return (grad_queries, grad_keys, grad_values)

    own_valid = key_valid(own_index * frame_count, frame_count)
    own_q, own_k, own_v = block_grads(queries, grad_attn, log_total, delta, keys, values, own_valid)

    def pass_grads(pair):
        return (
            from_behind(pair[0].astype(jnp.bfloat16), "blk", 1).astype(jnp.float32),
            from_behind(pair[1].astype(jnp.bfloat16), "blk", 1).astype(jnp.float32),
        )

    def keys_turn(step, carry):
        key_flat, value_flat, grad_key_flat, grad_value_flat, grad_query = carry
        key_flat, value_flat = from_behind((key_flat, value_flat), "blk", 1)
        grad_key_flat, grad_value_flat = pass_grads((grad_key_flat, grad_value_flat))
        owner = (own_index - step) % cycle_size
        part_q, part_k, part_v = block_grads(
            queries,
            grad_attn,
            log_total,
            delta,
            split_heads(key_flat),
            split_heads(value_flat),
            key_valid(owner * frame_count, frame_count),
        )
        return (
            key_flat,
            value_flat,
            grad_key_flat + join_heads(part_k),
            grad_value_flat + join_heads(part_v),
            grad_query + part_q,
        )

    loop_out = lax.fori_loop(
        1,
        cycle_size,
        keys_turn,
        (keys_flat, values_flat, join_heads(own_k), join_heads(own_v), own_q),
    )
    grad_key_flat, grad_value_flat = pass_grads((loop_out[2], loop_out[3]))
    grad_query = loop_out[4]
    grad_key = split_heads(grad_key_flat)
    grad_value = split_heads(grad_value_flat)
    grad_query = turn(grad_query, cosines, sines, -1.0)
    grad_key = turn(grad_key, cosines, sines, -1.0)
    grad_qkv = (
        jnp.stack([grad_query, grad_key, grad_value], axis=2)
        .astype(jnp.bfloat16)
        .reshape(-1, 3 * width)
    )
    grad_w_qkv = jnp.dot(hidden_a.T, grad_qkv, preferred_element_type=jnp.float32)
    grad_b_qkv = jnp.sum(grad_qkv.astype(jnp.float32), axis=0)
    grad_hidden_a = row_product(grad_qkv, w_qkv).reshape(seq_count, frame_count, width)
    grad_scale_a = jnp.sum(grad_hidden_a * norm_a, axis=1)
    grad_shift_a = jnp.sum(grad_hidden_a, axis=1)
    grad_inputs = grad_mixed + norm_back(norm_a, inverse_a, grad_hidden_a * (1.0 + scale_a))
    grad_mods = jnp.concatenate(
        [grad_shift_a, grad_scale_a, grad_gate_a, grad_shift_f, grad_scale_f, grad_gate_f], axis=-1
    )
    grad_w_mod = jnp.dot(
        time_act.astype(jnp.float32).T,
        grad_mods,
        precision=HIGH,
        preferred_element_type=jnp.float32,
    )
    grad_b_mod = jnp.sum(grad_mods, axis=0)
    full_mods = lax.psum(grad_mods, "blk")
    grad_silu = jnp.dot(
        full_mods, w_mod.astype(jnp.float32).T, precision=HIGH, preferred_element_type=jnp.float32
    )
    grad_time = silu_pull(grad_silu)[0]
    shares = (
        lax.psum_scatter(grad_w_mod, "blk", scatter_dimension=0, tiled=True),
        lax.psum_scatter(grad_b_mod, "blk", scatter_dimension=0, tiled=True),
        lax.psum_scatter(grad_w_qkv, "blk", scatter_dimension=0, tiled=True),
        lax.psum_scatter(grad_b_qkv, "blk", scatter_dimension=0, tiled=True),
        lax.psum_scatter(grad_w_out, "blk", scatter_dimension=0, tiled=True),
        lax.psum_scatter(grad_b_out, "blk", scatter_dimension=0, tiled=True),
        lax.psum_scatter(grad_w_up, "blk", scatter_dimension=0, tiled=True),
        lax.psum_scatter(grad_b_up, "blk", scatter_dimension=0, tiled=True),
        lax.psum_scatter(grad_w_down, "blk", scatter_dimension=0, tiled=True),
        lax.psum_scatter(grad_b_down, "blk", scatter_dimension=0, tiled=True),
    )
    shares = (
        lax.psum(shares[0].astype(jnp.bfloat16), "batch").astype(jnp.float32),
        lax.psum(shares[1].astype(jnp.bfloat16), "batch").astype(jnp.float32),
        lax.psum(shares[2].astype(jnp.bfloat16), "batch").astype(jnp.float32),
        lax.psum(shares[3].astype(jnp.bfloat16), "batch").astype(jnp.float32),
        lax.psum(shares[4].astype(jnp.bfloat16), "batch").astype(jnp.float32),
        lax.psum(shares[5].astype(jnp.bfloat16), "batch").astype(jnp.float32),
        lax.psum(shares[6].astype(jnp.bfloat16), "batch").astype(jnp.float32),
        lax.psum(shares[7].astype(jnp.bfloat16), "batch").astype(jnp.float32),
        lax.psum(shares[8].astype(jnp.bfloat16), "batch").astype(jnp.float32),
        lax.psum(shares[9].astype(jnp.bfloat16), "batch").astype(jnp.float32),
    )
    return (
        output,
        grad_inputs,
        grad_time,
        shares[0],
        shares[1],
        shares[2],
        shares[3],
        shares[4],
        shares[5],
        shares[6],
        shares[7],
        shares[8],
        shares[9],
    )


def solution(mesh):
    return jax.shard_map(
        on_device,
        mesh=mesh,
        in_specs=(
            P("batch", "blk", None),
            P("batch", None),
            P("batch"),
            P("batch", "blk", None),
            P(),
            P(),
            P(),
            P(),
            P(),
            P(),
            P(),
            P(),
            P(),
            P(),
        ),
        out_specs=(
            P("batch", "blk", None),
            P("batch", "blk", None),
            P("batch", None),
            P("blk", None),
            P("blk"),
            P("blk", None),
            P("blk"),
            P("blk", None),
            P("blk"),
            P("blk", None),
            P("blk"),
            P("blk", None),
            P("blk"),
        ),
        check_vma=False,
    )
```

profile of v0, /device:TPU:0, one launch (start us, length us, event | category | flops | bytes accessed | tf_op | source)
XLA Modules:
  0.0 1676.1 jit_solution(3099850114334731655)
XLA Ops:
  11.5 6.8 convolution_add_fusion.1
  23.8 5.7 reshape.396
  32.2 4.7 fusion.80
  52.7 204.2 %while.46 = (s32[]{:T(128)}, bf16[2,128,1024]{1,2,0:T(8,128)(2,1)}, bf16[2,128,1024]{1,2,0:T(8,128)(2,1)}, f32[2,16,128]{2,1,0:T(8,128)S(1)}, f32[2,16,128]{2,1,...) while((s32[]{:T(128)}, bf16[2,128,1024]{1,2,0:T(8,128)(2,1)}, ...), condition=%wide.region_7.8_spmd, body=%wide.region_4.7_spmd.sunk | while | flops 140517776 | bytes 24906140 | solution.py:155
  57.3 14.5 collective-permute-done
  74.2 7.8 collective-permute-done.1
  86.8 16.7 collective-permute-done
  106.0 6.9 collective-permute-done.1
  116.6 17.8 %collective-permute-done = bf16[2,128,1024]{1,2,0:T(8,128)(2,1)} collective-permute-done((bf16[2,128,1024]{1,2,0:T(8,128)(2,1)}, bf16[2,128,1024]{1,2,0:T(8,128)(2,1)}, u32[]{:S(2)}, u32[]{:S(2)}) %collective-permute-start) | collective-permute-done | bytes 524320 | tf_op jit(solution)/shard_map/while/body/eval_jaxpr/ppermute | solution.py:19
  136.8 6.0 collective-permute-done.1
  146.5 17.8 %collective-permute-done = bf16[2,128,1024]{1,2,0:T(8,128)(2,1)} collective-permute-done((bf16[2,128,1024]{1,2,0:T(8,128)(2,1)}, bf16[2,128,1024]{1,2,0:T(8,128)(2,1)}, u32[]{:S(2)}, u32[]{:S(2)}) %collective-permute-start) | collective-permute-done | bytes 524320 | tf_op jit(solution)/shard_map/while/body/eval_jaxpr/ppermute | solution.py:19
  166.7 5.1 collective-permute-done.1
  175.5 17.8 %collective-permute-done = bf16[2,128,1024]{1,2,0:T(8,128)(2,1)} collective-permute-done((bf16[2,128,1024]{1,2,0:T(8,128)(2,1)}, bf16[2,128,1024]{1,2,0:T(8,128)(2,1)}, u32[]{:S(2)}, u32[]{:S(2)}) %collective-permute-start) | collective-permute-done | bytes 524320 | tf_op jit(solution)/shard_map/while/body/eval_jaxpr/ppermute | solution.py:19
  195.7 4.2 collective-permute-done.1
  203.5 17.8 %collective-permute-done = bf16[2,128,1024]{1,2,0:T(8,128)(2,1)} collective-permute-done((bf16[2,128,1024]{1,2,0:T(8,128)(2,1)}, bf16[2,128,1024]{1,2,0:T(8,128)(2,1)}, u32[]{:S(2)}, u32[]{:S(2)}) %collective-permute-start) | collective-permute-done | bytes 524320 | tf_op jit(solution)/shard_map/while/body/eval_jaxpr/ppermute | solution.py:19
  230.6 17.0 %collective-permute-done = bf16[2,128,1024]{1,2,0:T(8,128)(2,1)} collective-permute-done((bf16[2,128,1024]{1,2,0:T(8,128)(2,1)}, bf16[2,128,1024]{1,2,0:T(8,128)(2,1)}, u32[]{:S(2)}, u32[]{:S(2)}) %collective-permute-start) | collective-permute-done | bytes 524320 | tf_op jit(solution)/shard_map/while/body/eval_jaxpr/ppermute | solution.py:19
  277.3 6.4 fusion.76
  284.2 6.0 fusion.84
  301.7 571.2 %while.47 = (s32[]{:T(128)}, bf16[2,128,1024]{1,2,0:T(8,128)(2,1)}, bf16[2,128,1024]{1,2,0:T(8,128)(2,1)}, bf16[2,128,1024]{1,2,0:T(8,128)(2,1)}, bf16[2,128,102...) while((s32[]{:T(128)}, bf16[2,128,1024]{1,2,0:T(8,128)(2,1)}, ...), condition=%wide.region_14.15_spmd, body=%wide.region_13.14_spmd.sunk | while | flops 341574016 | bytes 40404996 | solution.py:257
  301.9 28.7 %collective-permute-done.2 = bf16[2,128,1024]{1,2,0:T(8,128)(2,1)S(1)} collective-permute-done((bf16[2,128,1024]{1,2,0:T(8,128)(2,1)}, bf16[2,128,1024]{1,2,0:T(8,128)(2,1)S(1)}, u32[]{:S(2)}, u32[]{:S(2)}) %collective-permute-start.2) | collective-permute-done | bytes 524320 | tf_op jit(solution)/shard_map/while/body/eval_jaxpr/ppermute | solution.py:19
  331.7 32.7 %collective-permute-done.3 = bf16[2,128,1024]{1,2,0:T(8,128)(2,1)S(1)} collective-permute-done((bf16[2,128,1024]{1,2,0:T(8,128)(2,1)}, bf16[2,128,1024]{1,2,0:T(8,128)(2,1)S(1)}, u32[]{:S(2)}, u32[]{:S(2)}) %collective-permute-start.3) | collective-permute-done | bytes 524320 | tf_op jit(solution)/shard_map/while/body/eval_jaxpr/ppermute | solution.py:19
  376.3 14.6 collective-permute-done.2
  392.0 45.7 %collective-permute-done.3 = bf16[2,128,1024]{1,2,0:T(8,128)(2,1)S(1)} collective-permute-done((bf16[2,128,1024]{1,2,0:T(8,128)(2,1)}, bf16[2,128,1024]{1,2,0:T(8,128)(2,1)S(1)}, u32[]{:S(2)}, u32[]{:S(2)}) %collective-permute-start.3) | collective-permute-done | bytes 524320 | tf_op jit(solution)/shard_map/while/body/eval_jaxpr/ppermute | solution.py:19
  449.6 26.0 %collective-permute-done.2 = bf16[2,128,1024]{1,2,0:T(8,128)(2,1)S(1)} collective-permute-done((bf16[2,128,1024]{1,2,0:T(8,128)(2,1)}, bf16[2,128,1024]{1,2,0:T(8,128)(2,1)S(1)}, u32[]{:S(2)}, u32[]{:S(2)}) %collective-permute-start.2) | collective-permute-done | bytes 524320 | tf_op jit(solution)/shard_map/while/body/eval_jaxpr/ppermute | solution.py:19
  476.7 64.7 %collective-permute-done.3 = bf16[2,128,1024]{1,2,0:T(8,128)(2,1)S(1)} collective-permute-done((bf16[2,128,1024]{1,2,0:T(8,128)(2,1)}, bf16[2,128,1024]{1,2,0:T(8,128)(2,1)S(1)}, u32[]{:S(2)}, u32[]{:S(2)}) %collective-permute-start.3) | collective-permute-done | bytes 524320 | tf_op jit(solution)/shard_map/while/body/eval_jaxpr/ppermute | solution.py:19
  550.2 11.8 collective-permute-start.4
  566.2 5.6 collective-permute-done.2
  572.8 30.7 %collective-permute-done.3 = bf16[2,128,1024]{1,2,0:T(8,128)(2,1)S(1)} collective-permute-done((bf16[2,128,1024]{1,2,0:T(8,128)(2,1)}, bf16[2,128,1024]{1,2,0:T(8,128)(2,1)S(1)}, u32[]{:S(2)}, u32[]{:S(2)}) %collective-permute-start.3) | collective-permute-done | bytes 524320 | tf_op jit(solution)/shard_map/while/body/eval_jaxpr/ppermute | solution.py:19
  612.7 5.1 collective-permute-start.4
  617.9 5.6 collective-permute-start.3
  623.6 24.0 %collective-permute-done.2 = bf16[2,128,1024]{1,2,0:T(8,128)(2,1)S(1)} collective-permute-done((bf16[2,128,1024]{1,2,0:T(8,128)(2,1)}, bf16[2,128,1024]{1,2,0:T(8,128)(2,1)S(1)}, u32[]{:S(2)}, u32[]{:S(2)}) %collective-permute-start.2) | collective-permute-done | bytes 524320 | tf_op jit(solution)/shard_map/while/body/eval_jaxpr/ppermute | solution.py:19
  648.6 30.6 %collective-permute-done.3 = bf16[2,128,1024]{1,2,0:T(8,128)(2,1)S(1)} collective-permute-done((bf16[2,128,1024]{1,2,0:T(8,128)(2,1)}, bf16[2,128,1024]{1,2,0:T(8,128)(2,1)S(1)}, u32[]{:S(2)}, u32[]{:S(2)}) %collective-permute-start.3) | collective-permute-done | bytes 524320 | tf_op jit(solution)/shard_map/while/body/eval_jaxpr/ppermute | solution.py:19
  688.3 28.9 %collective-permute-done.2 = bf16[2,128,1024]{1,2,0:T(8,128)(2,1)S(1)} collective-permute-done((bf16[2,128,1024]{1,2,0:T(8,128)(2,1)}, bf16[2,128,1024]{1,2,0:T(8,128)(2,1)S(1)}, u32[]{:S(2)}, u32[]{:S(2)}) %collective-permute-start.2) | collective-permute-done | bytes 524320 | tf_op jit(solution)/shard_map/while/body/eval_jaxpr/ppermute | solution.py:19
  718.2 41.3 %collective-permute-done.3 = bf16[2,128,1024]{1,2,0:T(8,128)(2,1)S(1)} collective-permute-done((bf16[2,128,1024]{1,2,0:T(8,128)(2,1)}, bf16[2,128,1024]{1,2,0:T(8,128)(2,1)S(1)}, u32[]{:S(2)}, u32[]{:S(2)}) %collective-permute-start.3) | collective-permute-done | bytes 524320 | tf_op jit(solution)/shard_map/while/body/eval_jaxpr/ppermute | solution.py:19
  771.3 26.1 %collective-permute-done.2 = bf16[2,128,1024]{1,2,0:T(8,128)(2,1)S(1)} collective-permute-done((bf16[2,128,1024]{1,2,0:T(8,128)(2,1)}, bf16[2,128,1024]{1,2,0:T(8,128)(2,1)S(1)}, u32[]{:S(2)}, u32[]{:S(2)}) %collective-permute-start.2) | collective-permute-done | bytes 524320 | tf_op jit(solution)/shard_map/while/body/eval_jaxpr/ppermute | solution.py:19
  798.5 65.6 %collective-permute-done.3 = bf16[2,128,1024]{1,2,0:T(8,128)(2,1)S(1)} collective-permute-done((bf16[2,128,1024]{1,2,0:T(8,128)(2,1)}, bf16[2,128,1024]{1,2,0:T(8,128)(2,1)S(1)}, u32[]{:S(2)}, u32[]{:S(2)}) %collective-permute-start.3) | collective-permute-done | bytes 524320 | tf_op jit(solution)/shard_map/while/body/eval_jaxpr/ppermute | solution.py:19
  873.1 17.6 %collective-permute-done.6 = bf16[2,128,1024]{1,2,0:T(8,128)(2,1)S(1)} collective-permute-done((bf16[2,128,1024]{1,2,0:T(8,128)(2,1)}, bf16[2,128,1024]{1,2,0:T(8,128)(2,1)S(1)}, u32[]{:S(2)}, u32[]{:S(2)}) %collective-permute-start.6) | collective-permute-done | bytes 524320 | tf_op jit(solution)/shard_map/ppermute | solution.py:19
  891.4 7.6 collective-permute-done.7
  901.1 6.5 fusion.26
  907.9 5.2 fusion.42
  914.7 13.4 fusion.68
  932.1 30.5 %reduce-scatter.12.cloned.1.call-done = f32[128,2048]{1,0:T(8,128)} async-done(((f32[1024,2048]{1,0:T(8,128)}), f32[128,2048]{1,0:T(8,128)}) %reduce-scatter.12.cloned.1.call-update) | async-done | bytes 1048592 | tf_op jit(solution)/shard_map/reduce_scatter | solution.py:302
  964.6 208.1 %reduce-scatter.8.cloned.1.call-done = f32[128,3072]{1,0:T(8,128)} async-done(((f32[1024,3072]{1,0:T(8,128)}), f32[128,3072]{1,0:T(8,128)}) %reduce-scatter.8.cloned.1.call-update) | async-done | bytes 1572880 | tf_op jit(solution)/shard_map/reduce_scatter | solution.py:298
  1175.1 404.8 %reduce-scatter.6.cloned.1.call-done = f32[128,6144]{1,0:T(8,128)} async-done(((f32[1024,6144]{1,0:T(8,128)}), f32[128,6144]{1,0:T(8,128)}) %reduce-scatter.6.cloned.1.call-update) | async-done | bytes 3145744 | tf_op jit(solution)/shard_map/reduce_scatter | solution.py:296
  1587.1 36.6 %all-reduce.12 = (f32[2,6144]{1,0:T(2,128)S(1)}, bf16[6144]{0:T(1024)(128)(2,1)S(1)}, bf16[3072]{0:T(1024)(128)(2,1)S(1)}, bf16[1024]{0:T(1024)(128)(2,1)S(1)}, ...) all-reduce(f32[2,6144]{1,0:T(2,128)S(1)} %constant_dynamic-update-s, ...), channel_id=1, replica_groups=mesh['batch'=4,'blk'=8] {'blk'}, use_global_device_ids=true, to_apply=%region_23.24 | all-reduce | flops 25600 | bytes 178176 | tf_op jit(solution)/shard_map/psum | solution.py:290
  1624.0 5.9 all-reduce.6
  1632.8 13.4 fusion.66
  1646.2 14.4 all-reduce.11.cloned.1.call-done
  (463 shorter events, 226.8 us)
Async XLA Ops:
  7.2 921.0 %reduce-scatter.10.cloned.1.call-start = ((), (), s32[]{:S(2)}) async-start(), calls=%async_computation.7 | async-start | bytes 4718592 | tf_op jit(solution)/shard_map/reduce_scatter | solution.py:300
  52.7 19.1 %collective-permute-start = (bf16[2,128,1024]{1,2,0:T(8,128)(2,1)}, bf16[2,128,1024]{1,2,0:T(8,128)(2,1)}, u32[]{:S(2)}, u32[]{:S(2)}) collective-permute-start(bf16[2,128,1024]{1,2,0:T(8,128)(2,1)} %get-tuple-element.847), channel_id=1, source_target_pairs={{7,0},{0,1},{1,2},{2,3},{3,4},{4,5},{5,6},{6,7},{15,8},{8,9},{9,10... | collective-permute-start | bytes 1572872 | tf_op jit(solution)/shard_map/while/body/eval_jaxpr/ppermute | solution.py:19
  55.7 26.4 %collective-permute-start.1 = (bf16[2,128,1024]{1,2,0:T(8,128)(2,1)}, bf16[2,128,1024]{1,2,0:T(8,128)(2,1)S(1)}, u32[]{:S(2)}, u32[]{:S(2)}) collective-permute-start(bf16[2,128,1024]{1,2,0:T(8,128)(2,1)} %get-tuple-element.848), channel_id=1, source_target_pairs={{7,0},{0,1},{1,2},{2,3},{3,4},{4,5},{5,6},{6,7},{15,8},{8,9},{9,10... | collective-permute-start | bytes 1572872 | tf_op jit(solution)/shard_map/while/body/eval_jaxpr/ppermute | solution.py:19
  85.6 17.9 %collective-permute-start = (bf16[2,128,1024]{1,2,0:T(8,128)(2,1)}, bf16[2,128,1024]{1,2,0:T(8,128)(2,1)}, u32[]{:S(2)}, u32[]{:S(2)}) collective-permute-start(bf16[2,128,1024]{1,2,0:T(8,128)(2,1)} %get-tuple-element.847), channel_id=1, source_target_pairs={{7,0},{0,1},{1,2},{2,3},{3,4},{4,5},{5,6},{6,7},{15,8},{8,9},{9,10... | collective-permute-start | bytes 1572872 | tf_op jit(solution)/shard_map/while/body/eval_jaxpr/ppermute | solution.py:19
  85.6 27.2 %collective-permute-start.1 = (bf16[2,128,1024]{1,2,0:T(8,128)(2,1)}, bf16[2,128,1024]{1,2,0:T(8,128)(2,1)S(1)}, u32[]{:S(2)}, u32[]{:S(2)}) collective-permute-start(bf16[2,128,1024]{1,2,0:T(8,128)(2,1)} %get-tuple-element.848), channel_id=1, source_target_pairs={{7,0},{0,1},{1,2},{2,3},{3,4},{4,5},{5,6},{6,7},{15,8},{8,9},{9,10... | collective-permute-start | bytes 1572872 | tf_op jit(solution)/shard_map/while/body/eval_jaxpr/ppermute | solution.py:19
  116.5 17.9 %collective-permute-start = (bf16[2,128,1024]{1,2,0:T(8,128)(2,1)}, bf16[2,128,1024]{1,2,0:T(8,128)(2,1)}, u32[]{:S(2)}, u32[]{:S(2)}) collective-permute-start(bf16[2,128,1024]{1,2,0:T(8,128)(2,1)} %get-tuple-element.847), channel_id=1, source_target_pairs={{7,0},{0,1},{1,2},{2,3},{3,4},{4,5},{5,6},{6,7},{15,8},{8,9},{9,10... | collective-permute-start | bytes 1572872 | tf_op jit(solution)/shard_map/while/body/eval_jaxpr/ppermute | solution.py:19
  116.5 26.3 %collective-permute-start.1 = (bf16[2,128,1024]{1,2,0:T(8,128)(2,1)}, bf16[2,128,1024]{1,2,0:T(8,128)(2,1)S(1)}, u32[]{:S(2)}, u32[]{:S(2)}) collective-permute-start(bf16[2,128,1024]{1,2,0:T(8,128)(2,1)} %get-tuple-element.848), channel_id=1, source_target_pairs={{7,0},{0,1},{1,2},{2,3},{3,4},{4,5},{5,6},{6,7},{15,8},{8,9},{9,10... | collective-permute-start | bytes 1572872 | tf_op jit(solution)/shard_map/while/body/eval_jaxpr/ppermute | solution.py:19
  146.4 17.9 %collective-permute-start = (bf16[2,128,1024]{1,2,0:T(8,128)(2,1)}, bf16[2,128,1024]{1,2,0:T(8,128)(2,1)}, u32[]{:S(2)}, u32[]{:S(2)}) collective-permute-start(bf16[2,128,1024]{1,2,0:T(8,128)(2,1)} %get-tuple-element.847), channel_id=1, source_target_pairs={{7,0},{0,1},{1,2},{2,3},{3,4},{4,5},{5,6},{6,7},{15,8},{8,9},{9,10... | collective-permute-start | bytes 1572872 | tf_op jit(solution)/shard_map/while/body/eval_jaxpr/ppermute | solution.py:19
  146.4 25.4 %collective-permute-start.1 = (bf16[2,128,1024]{1,2,0:T(8,128)(2,1)}, bf16[2,128,1024]{1,2,0:T(8,128)(2,1)S(1)}, u32[]{:S(2)}, u32[]{:S(2)}) collective-permute-start(bf16[2,128,1024]{1,2,0:T(8,128)(2,1)} %get-tuple-element.848), channel_id=1, source_target_pairs={{7,0},{0,1},{1,2},{2,3},{3,4},{4,5},{5,6},{6,7},{15,8},{8,9},{9,10... | collective-permute-start | bytes 1572872 | tf_op jit(solution)/shard_map/while/body/eval_jaxpr/ppermute | solution.py:19
  175.3 17.9 %collective-permute-start = (bf16[2,128,1024]{1,2,0:T(8,128)(2,1)}, bf16[2,128,1024]{1,2,0:T(8,128)(2,1)}, u32[]{:S(2)}, u32[]{:S(2)}) collective-permute-start(bf16[2,128,1024]{1,2,0:T(8,128)(2,1)} %get-tuple-element.847), channel_id=1, source_target_pairs={{7,0},{0,1},{1,2},{2,3},{3,4},{4,5},{5,6},{6,7},{15,8},{8,9},{9,10... | collective-permute-start | bytes 1572872 | tf_op jit(solution)/shard_map/while/body/eval_jaxpr/ppermute | solution.py:19
  175.3 24.5 %collective-permute-start.1 = (bf16[2,128,1024]{1,2,0:T(8,128)(2,1)}, bf16[2,128,1024]{1,2,0:T(8,128)(2,1)S(1)}, u32[]{:S(2)}, u32[]{:S(2)}) collective-permute-start(bf16[2,128,1024]{1,2,0:T(8,128)(2,1)} %get-tuple-element.848), channel_id=1, source_target_pairs={{7,0},{0,1},{1,2},{2,3},{3,4},{4,5},{5,6},{6,7},{15,8},{8,9},{9,10... | collective-permute-start | bytes 1572872 | tf_op jit(solution)/shard_map/while/body/eval_jaxpr/ppermute | solution.py:19
  203.4 17.9 %collective-permute-start = (bf16[2,128,1024]{1,2,0:T(8,128)(2,1)}, bf16[2,128,1024]{1,2,0:T(8,128)(2,1)}, u32[]{:S(2)}, u32[]{:S(2)}) collective-permute-start(bf16[2,128,1024]{1,2,0:T(8,128)(2,1)} %get-tuple-element.847), channel_id=1, source_target_pairs={{7,0},{0,1},{1,2},{2,3},{3,4},{4,5},{5,6},{6,7},{15,8},{8,9},{9,10... | collective-permute-start | bytes 1572872 | tf_op jit(solution)/shard_map/while/body/eval_jaxpr/ppermute | solution.py:19
  203.4 23.6 %collective-permute-start.1 = (bf16[2,128,1024]{1,2,0:T(8,128)(2,1)}, bf16[2,128,1024]{1,2,0:T(8,128)(2,1)S(1)}, u32[]{:S(2)}, u32[]{:S(2)}) collective-permute-start(bf16[2,128,1024]{1,2,0:T(8,128)(2,1)} %get-tuple-element.848), channel_id=1, source_target_pairs={{7,0},{0,1},{1,2},{2,3},{3,4},{4,5},{5,6},{6,7},{15,8},{8,9},{9,10... | collective-permute-start | bytes 1572872 | tf_op jit(solution)/shard_map/while/body/eval_jaxpr/ppermute | solution.py:19
  230.5 22.6 %collective-permute-start.1 = (bf16[2,128,1024]{1,2,0:T(8,128)(2,1)}, bf16[2,128,1024]{1,2,0:T(8,128)(2,1)S(1)}, u32[]{:S(2)}, u32[]{:S(2)}) collective-permute-start(bf16[2,128,1024]{1,2,0:T(8,128)(2,1)} %get-tuple-element.848), channel_id=1, source_target_pairs={{7,0},{0,1},{1,2},{2,3},{3,4},{4,5},{5,6},{6,7},{15,8},{8,9},{9,10... | collective-permute-start | bytes 1572872 | tf_op jit(solution)/shard_map/while/body/eval_jaxpr/ppermute | solution.py:19
  277.3 652.7 %reduce-scatter.14.cloned.1.call-start = ((), (), s32[]{:S(2)}) async-start(), calls=%async_computation.9 | async-start | bytes 9437184 | tf_op jit(solution)/shard_map/reduce_scatter | solution.py:304
  283.8 678.7 %reduce-scatter.12.cloned.1.call-start = ((), (), s32[]{:S(2)}) async-start(), calls=%async_computation.8 | async-start | bytes 9437184 | tf_op jit(solution)/shard_map/reduce_scatter | solution.py:302
  290.2 882.4 %reduce-scatter.8.cloned.1.call-start = ((), (), s32[]{:S(2)}) async-start(), calls=%async_computation.6 | async-start | bytes 14155776 | tf_op jit(solution)/shard_map/reduce_scatter | solution.py:298
  301.7 28.9 %collective-permute-start.2 = (bf16[2,128,1024]{1,2,0:T(8,128)(2,1)}, bf16[2,128,1024]{1,2,0:T(8,128)(2,1)S(1)}, u32[]{:S(2)}, u32[]{:S(2)}) collective-permute-start(bf16[2,128,1024]{1,2,0:T(8,128)(2,1)} %get-tuple-element.892), channel_id=1, source_target_pairs={{7,0},{0,1},{1,2},{2,3},{3,4},{4,5},{5,6},{6,7},{15,8},{8,9},{9,10... | collective-permute-start | bytes 1572872 | tf_op jit(solution)/shard_map/while/body/eval_jaxpr/ppermute | solution.py:19
  301.7 66.2 %collective-permute-start.5 = (bf16[2,128,1024]{1,2,0:T(8,128)(2,1)}, bf16[2,128,1024]{1,2,0:T(8,128)(2,1)}, u32[]{:S(2)}, u32[]{:S(2)}) collective-permute-start(bf16[2,128,1024]{1,2,0:T(8,128)(2,1)} %get-tuple-element.895), channel_id=1, source_target_pairs={{7,0},{0,1},{1,2},{2,3},{3,4},{4,5},{5,6},{6,7},{15,8},{8,9},{9,10... | collective-permute-start | bytes 1572872 | tf_op jit(solution)/shard_map/while/body/eval_jaxpr/ppermute | solution.py:19
  301.7 69.1 %collective-permute-start.4 = (bf16[2,128,1024]{1,2,0:T(8,128)(2,1)}, bf16[2,128,1024]{1,2,0:T(8,128)(2,1)}, u32[]{:S(2)}, u32[]{:S(2)}) collective-permute-start(bf16[2,128,1024]{1,2,0:T(8,128)(2,1)} %get-tuple-element.894), channel_id=1, source_target_pairs={{7,0},{0,1},{1,2},{2,3},{3,4},{4,5},{5,6},{6,7},{15,8},{8,9},{9,10... | collective-permute-start | bytes 1572872 | tf_op jit(solution)/shard_map/while/body/eval_jaxpr/ppermute | solution.py:19
  301.8 62.6 %collective-permute-start.3 = (bf16[2,128,1024]{1,2,0:T(8,128)(2,1)}, bf16[2,128,1024]{1,2,0:T(8,128)(2,1)S(1)}, u32[]{:S(2)}, u32[]{:S(2)}) collective-permute-start(bf16[2,128,1024]{1,2,0:T(8,128)(2,1)} %get-tuple-element.893), channel_id=1, source_target_pairs={{7,0},{0,1},{1,2},{2,3},{3,4},{4,5},{5,6},{6,7},{15,8},{8,9},{9,10... | collective-permute-start | bytes 1572872 | tf_op jit(solution)/shard_map/while/body/eval_jaxpr/ppermute | solution.py:19
  373.2 68.1 %collective-permute-start.5 = (bf16[2,128,1024]{1,2,0:T(8,128)(2,1)}, bf16[2,128,1024]{1,2,0:T(8,128)(2,1)}, u32[]{:S(2)}, u32[]{:S(2)}) collective-permute-start(bf16[2,128,1024]{1,2,0:T(8,128)(2,1)} %get-tuple-element.895), channel_id=1, source_target_pairs={{7,0},{0,1},{1,2},{2,3},{3,4},{4,5},{5,6},{6,7},{15,8},{8,9},{9,10... | collective-permute-start | bytes 1572872 | tf_op jit(solution)/shard_map/while/body/eval_jaxpr/ppermute | solution.py:19
  373.3 71.0 %collective-permute-start.4 = (bf16[2,128,1024]{1,2,0:T(8,128)(2,1)}, bf16[2,128,1024]{1,2,0:T(8,128)(2,1)}, u32[]{:S(2)}, u32[]{:S(2)}) collective-permute-start(bf16[2,128,1024]{1,2,0:T(8,128)(2,1)} %get-tuple-element.894), channel_id=1, source_target_pairs={{7,0},{0,1},{1,2},{2,3},{3,4},{4,5},{5,6},{6,7},{15,8},{8,9},{9,10... | collective-permute-start | bytes 1572872 | tf_op jit(solution)/shard_map/while/body/eval_jaxpr/ppermute | solution.py:19
  373.4 64.3 %collective-permute-start.3 = (bf16[2,128,1024]{1,2,0:T(8,128)(2,1)}, bf16[2,128,1024]{1,2,0:T(8,128)(2,1)S(1)}, u32[]{:S(2)}, u32[]{:S(2)}) collective-permute-start(bf16[2,128,1024]{1,2,0:T(8,128)(2,1)} %get-tuple-element.893), channel_id=1, source_target_pairs={{7,0},{0,1},{1,2},{2,3},{3,4},{4,5},{5,6},{6,7},{15,8},{8,9},{9,10... | collective-permute-start | bytes 1572872 | tf_op jit(solution)/shard_map/while/body/eval_jaxpr/ppermute | solution.py:19
  446.6 28.9 %collective-permute-start.2 = (bf16[2,128,1024]{1,2,0:T(8,128)(2,1)}, bf16[2,128,1024]{1,2,0:T(8,128)(2,1)S(1)}, u32[]{:S(2)}, u32[]{:S(2)}) collective-permute-start(bf16[2,128,1024]{1,2,0:T(8,128)(2,1)} %get-tuple-element.892), channel_id=1, source_target_pairs={{7,0},{0,1},{1,2},{2,3},{3,4},{4,5},{5,6},{6,7},{15,8},{8,9},{9,10... | collective-permute-start | bytes 1572872 | tf_op jit(solution)/shard_map/while/body/eval_jaxpr/ppermute | solution.py:19
  446.7 98.3 %collective-permute-start.5 = (bf16[2,128,1024]{1,2,0:T(8,128)(2,1)}, bf16[2,128,1024]{1,2,0:T(8,128)(2,1)}, u32[]{:S(2)}, u32[]{:S(2)}) collective-permute-start(bf16[2,128,1024]{1,2,0:T(8,128)(2,1)} %get-tuple-element.895), channel_id=1, source_target_pairs={{7,0},{0,1},{1,2},{2,3},{3,4},{4,5},{5,6},{6,7},{15,8},{8,9},{9,10... | collective-permute-start | bytes 1572872 | tf_op jit(solution)/shard_map/while/body/eval_jaxpr/ppermute | solution.py:19
  446.7 101.2 %collective-permute-start.4 = (bf16[2,128,1024]{1,2,0:T(8,128)(2,1)}, bf16[2,128,1024]{1,2,0:T(8,128)(2,1)}, u32[]{:S(2)}, u32[]{:S(2)}) collective-permute-start(bf16[2,128,1024]{1,2,0:T(8,128)(2,1)} %get-tuple-element.894), channel_id=1, source_target_pairs={{7,0},{0,1},{1,2},{2,3},{3,4},{4,5},{5,6},{6,7},{15,8},{8,9},{9,10... | collective-permute-start | bytes 1572872 | tf_op jit(solution)/shard_map/while/body/eval_jaxpr/ppermute | solution.py:19
  446.7 94.6 %collective-permute-start.3 = (bf16[2,128,1024]{1,2,0:T(8,128)(2,1)}, bf16[2,128,1024]{1,2,0:T(8,128)(2,1)S(1)}, u32[]{:S(2)}, u32[]{:S(2)}) collective-permute-start(bf16[2,128,1024]{1,2,0:T(8,128)(2,1)} %get-tuple-element.893), channel_id=1, source_target_pairs={{7,0},{0,1},{1,2},{2,3},{3,4},{4,5},{5,6},{6,7},{15,8},{8,9},{9,10... | collective-permute-start | bytes 1572872 | tf_op jit(solution)/shard_map/while/body/eval_jaxpr/ppermute | solution.py:19
  550.1 21.6 %collective-permute-start.2 = (bf16[2,128,1024]{1,2,0:T(8,128)(2,1)}, bf16[2,128,1024]{1,2,0:T(8,128)(2,1)S(1)}, u32[]{:S(2)}, u32[]{:S(2)}) collective-permute-start(bf16[2,128,1024]{1,2,0:T(8,128)(2,1)} %get-tuple-element.892), channel_id=1, source_target_pairs={{7,0},{0,1},{1,2},{2,3},{3,4},{4,5},{5,6},{6,7},{15,8},{8,9},{9,10... | collective-permute-start | bytes 1572872 | tf_op jit(solution)/shard_map/while/body/eval_jaxpr/ppermute | solution.py:19
  550.1 56.9 %collective-permute-start.5 = (bf16[2,128,1024]{1,2,0:T(8,128)(2,1)}, bf16[2,128,1024]{1,2,0:T(8,128)(2,1)}, u32[]{:S(2)}, u32[]{:S(2)}) collective-permute-start(bf16[2,128,1024]{1,2,0:T(8,128)(2,1)} %get-tuple-element.895), channel_id=1, source_target_pairs={{7,0},{0,1},{1,2},{2,3},{3,4},{4,5},{5,6},{6,7},{15,8},{8,9},{9,10... | collective-permute-start | bytes 1572872 | tf_op jit(solution)/shard_map/while/body/eval_jaxpr/ppermute | solution.py:19
  550.2 59.8 %collective-permute-start.4 = (bf16[2,128,1024]{1,2,0:T(8,128)(2,1)}, bf16[2,128,1024]{1,2,0:T(8,128)(2,1)}, u32[]{:S(2)}, u32[]{:S(2)}) collective-permute-start(bf16[2,128,1024]{1,2,0:T(8,128)(2,1)} %get-tuple-element.894), channel_id=1, source_target_pairs={{7,0},{0,1},{1,2},{2,3},{3,4},{4,5},{5,6},{6,7},{15,8},{8,9},{9,10... | collective-permute-start | bytes 1572872 | tf_op jit(solution)/shard_map/while/body/eval_jaxpr/ppermute | solution.py:19
  562.0 41.5 %collective-permute-start.3 = (bf16[2,128,1024]{1,2,0:T(8,128)(2,1)}, bf16[2,128,1024]{1,2,0:T(8,128)(2,1)S(1)}, u32[]{:S(2)}, u32[]{:S(2)}) collective-permute-start(bf16[2,128,1024]{1,2,0:T(8,128)(2,1)} %get-tuple-element.893), channel_id=1, source_target_pairs={{7,0},{0,1},{1,2},{2,3},{3,4},{4,5},{5,6},{6,7},{15,8},{8,9},{9,10... | collective-permute-start | bytes 1572872 | tf_op jit(solution)/shard_map/while/body/eval_jaxpr/ppermute | solution.py:19
  612.3 35.3 %collective-permute-start.2 = (bf16[2,128,1024]{1,2,0:T(8,128)(2,1)}, bf16[2,128,1024]{1,2,0:T(8,128)(2,1)S(1)}, u32[]{:S(2)}, u32[]{:S(2)}) collective-permute-start(bf16[2,128,1024]{1,2,0:T(8,128)(2,1)} %get-tuple-element.892), channel_id=1, source_target_pairs={{7,0},{0,1},{1,2},{2,3},{3,4},{4,5},{5,6},{6,7},{15,8},{8,9},{9,10... | collective-permute-start | bytes 1572872 | tf_op jit(solution)/shard_map/while/body/eval_jaxpr/ppermute | solution.py:19
  612.3 70.5 %collective-permute-start.5 = (bf16[2,128,1024]{1,2,0:T(8,128)(2,1)}, bf16[2,128,1024]{1,2,0:T(8,128)(2,1)}, u32[]{:S(2)}, u32[]{:S(2)}) collective-permute-start(bf16[2,128,1024]{1,2,0:T(8,128)(2,1)} %get-tuple-element.895), channel_id=1, source_target_pairs={{7,0},{0,1},{1,2},{2,3},{3,4},{4,5},{5,6},{6,7},{15,8},{8,9},{9,10... | collective-permute-start | bytes 1572872 | tf_op jit(solution)/shard_map/while/body/eval_jaxpr/ppermute | solution.py:19
  612.7 73.0 %collective-permute-start.4 = (bf16[2,128,1024]{1,2,0:T(8,128)(2,1)}, bf16[2,128,1024]{1,2,0:T(8,128)(2,1)}, u32[]{:S(2)}, u32[]{:S(2)}) collective-permute-start(bf16[2,128,1024]{1,2,0:T(8,128)(2,1)} %get-tuple-element.894), channel_id=1, source_target_pairs={{7,0},{0,1},{1,2},{2,3},{3,4},{4,5},{5,6},{6,7},{15,8},{8,9},{9,10... | collective-permute-start | bytes 1572872 | tf_op jit(solution)/shard_map/while/body/eval_jaxpr/ppermute | solution.py:19
  617.9 61.4 %collective-permute-start.3 = (bf16[2,128,1024]{1,2,0:T(8,128)(2,1)}, bf16[2,128,1024]{1,2,0:T(8,128)(2,1)S(1)}, u32[]{:S(2)}, u32[]{:S(2)}) collective-permute-start(bf16[2,128,1024]{1,2,0:T(8,128)(2,1)} %get-tuple-element.893), channel_id=1, source_target_pairs={{7,0},{0,1},{1,2},{2,3},{3,4},{4,5},{5,6},{6,7},{15,8},{8,9},{9,10... | collective-permute-start | bytes 1572872 | tf_op jit(solution)/shard_map/while/body/eval_jaxpr/ppermute | solution.py:19
  688.0 29.1 %collective-permute-start.2 = (bf16[2,128,1024]{1,2,0:T(8,128)(2,1)}, bf16[2,128,1024]{1,2,0:T(8,128)(2,1)S(1)}, u32[]{:S(2)}, u32[]{:S(2)}) collective-permute-start(bf16[2,128,1024]{1,2,0:T(8,128)(2,1)} %get-tuple-element.892), channel_id=1, source_target_pairs={{7,0},{0,1},{1,2},{2,3},{3,4},{4,5},{5,6},{6,7},{15,8},{8,9},{9,10... | collective-permute-start | bytes 1572872 | tf_op jit(solution)/shard_map/while/body/eval_jaxpr/ppermute | solution.py:19
  688.0 75.1 %collective-permute-start.5 = (bf16[2,128,1024]{1,2,0:T(8,128)(2,1)}, bf16[2,128,1024]{1,2,0:T(8,128)(2,1)}, u32[]{:S(2)}, u32[]{:S(2)}) collective-permute-start(bf16[2,128,1024]{1,2,0:T(8,128)(2,1)} %get-tuple-element.895), channel_id=1, source_target_pairs={{7,0},{0,1},{1,2},{2,3},{3,4},{4,5},{5,6},{6,7},{15,8},{8,9},{9,10... | collective-permute-start | bytes 1572872 | tf_op jit(solution)/shard_map/while/body/eval_jaxpr/ppermute | solution.py:19
  688.0 77.9 %collective-permute-start.4 = (bf16[2,128,1024]{1,2,0:T(8,128)(2,1)}, bf16[2,128,1024]{1,2,0:T(8,128)(2,1)}, u32[]{:S(2)}, u32[]{:S(2)}) collective-permute-start(bf16[2,128,1024]{1,2,0:T(8,128)(2,1)} %get-tuple-element.894), channel_id=1, source_target_pairs={{7,0},{0,1},{1,2},{2,3},{3,4},{4,5},{5,6},{6,7},{15,8},{8,9},{9,10... | collective-permute-start | bytes 1572872 | tf_op jit(solution)/shard_map/while/body/eval_jaxpr/ppermute | solution.py:19
  688.1 71.4 %collective-permute-start.3 = (bf16[2,128,1024]{1,2,0:T(8,128)(2,1)}, bf16[2,128,1024]{1,2,0:T(8,128)(2,1)S(1)}, u32[]{:S(2)}, u32[]{:S(2)}) collective-permute-start(bf16[2,128,1024]{1,2,0:T(8,128)(2,1)} %get-tuple-element.893), channel_id=1, source_target_pairs={{7,0},{0,1},{1,2},{2,3},{3,4},{4,5},{5,6},{6,7},{15,8},{8,9},{9,10... | collective-permute-start | bytes 1572872 | tf_op jit(solution)/shard_map/while/body/eval_jaxpr/ppermute | solution.py:19
  768.3 29.1 %collective-permute-start.2 = (bf16[2,128,1024]{1,2,0:T(8,128)(2,1)}, bf16[2,128,1024]{1,2,0:T(8,128)(2,1)S(1)}, u32[]{:S(2)}, u32[]{:S(2)}) collective-permute-start(bf16[2,128,1024]{1,2,0:T(8,128)(2,1)} %get-tuple-element.892), channel_id=1, source_target_pairs={{7,0},{0,1},{1,2},{2,3},{3,4},{4,5},{5,6},{6,7},{15,8},{8,9},{9,10... | collective-permute-start | bytes 1572872 | tf_op jit(solution)/shard_map/while/body/eval_jaxpr/ppermute | solution.py:19
  768.3 99.4 %collective-permute-start.5 = (bf16[2,128,1024]{1,2,0:T(8,128)(2,1)}, bf16[2,128,1024]{1,2,0:T(8,128)(2,1)}, u32[]{:S(2)}, u32[]{:S(2)}) collective-permute-start(bf16[2,128,1024]{1,2,0:T(8,128)(2,1)} %get-tuple-element.895), channel_id=1, source_target_pairs={{7,0},{0,1},{1,2},{2,3},{3,4},{4,5},{5,6},{6,7},{15,8},{8,9},{9,10... | collective-permute-start | bytes 1572872 | tf_op jit(solution)/shard_map/while/body/eval_jaxpr/ppermute | solution.py:19
  768.3 102.3 %collective-permute-start.4 = (bf16[2,128,1024]{1,2,0:T(8,128)(2,1)}, bf16[2,128,1024]{1,2,0:T(8,128)(2,1)}, u32[]{:S(2)}, u32[]{:S(2)}) collective-permute-start(bf16[2,128,1024]{1,2,0:T(8,128)(2,1)} %get-tuple-element.894), channel_id=1, source_target_pairs={{7,0},{0,1},{1,2},{2,3},{3,4},{4,5},{5,6},{6,7},{15,8},{8,9},{9,10... | collective-permute-start | bytes 1572872 | tf_op jit(solution)/shard_map/while/body/eval_jaxpr/ppermute | solution.py:19
  768.4 95.7 %collective-permute-start.3 = (bf16[2,128,1024]{1,2,0:T(8,128)(2,1)}, bf16[2,128,1024]{1,2,0:T(8,128)(2,1)S(1)}, u32[]{:S(2)}, u32[]{:S(2)}) collective-permute-start(bf16[2,128,1024]{1,2,0:T(8,128)(2,1)} %get-tuple-element.893), channel_id=1, source_target_pairs={{7,0},{0,1},{1,2},{2,3},{3,4},{4,5},{5,6},{6,7},{15,8},{8,9},{9,10... | collective-permute-start | bytes 1572872 | tf_op jit(solution)/shard_map/while/body/eval_jaxpr/ppermute | solution.py:19
  872.9 17.9 %collective-permute-start.6 = (bf16[2,128,1024]{1,2,0:T(8,128)(2,1)}, bf16[2,128,1024]{1,2,0:T(8,128)(2,1)S(1)}, u32[]{:S(2)}, u32[]{:S(2)}) collective-permute-start(bf16[2,128,1024]{1,2,0:T(8,128)(2,1)} %get-tuple-element.529), channel_id=1, source_target_pairs={{7,0},{0,1},{1,2},{2,3},{3,4},{4,5},{5,6},{6,7},{15,8},{8,9},{9,10... | collective-permute-start | bytes 1572872 | tf_op jit(solution)/shard_map/ppermute | solution.py:19
  872.9 26.1 %collective-permute-start.7 = (bf16[2,128,1024]{1,2,0:T(8,128)(2,1)}, bf16[2,128,1024]{1,2,0:T(8,128)(2,1)S(1)}, u32[]{:S(2)}, u32[]{:S(2)}) collective-permute-start(bf16[2,128,1024]{1,2,0:T(8,128)(2,1)} %get-tuple-element.530), channel_id=1, source_target_pairs={{7,0},{0,1},{1,2},{2,3},{3,4},{4,5},{5,6},{6,7},{15,8},{8,9},{9,10... | collective-permute-start | bytes 1572872 | tf_op jit(solution)/shard_map/ppermute | solution.py:19
  907.6 672.2 %reduce-scatter.6.cloned.1.call-start = ((), (), s32[]{:S(2)}) async-start(), calls=%async_computation.5 | async-start | bytes 28311552 | tf_op jit(solution)/shard_map/reduce_scatter | solution.py:296
  928.1 732.5 %all-reduce.11.cloned.1.call-start = ((), (), s32[]{:S(2)}) async-start(), calls=%async_computation.10 | async-start | bytes 7340032 | tf_op jit(solution)/shard_map/psum | solution.py:308
  (75 other events, 543.0 us)
Sparse Core Ops, SparseCore 0:
  277.4 140.6 reduce-scatter.9
  422.2 293.1 reduce-scatter.13
  719.1 243.3 reduce-scatter.11
  966.4 206.2 reduce-scatter.7
  1176.9 402.9 reduce-scatter.5
  1583.8 76.7 all-reduce.10
where the time goes:
time: 1690 us; the launch traced here: 1680 us
  waiting for transfers between devices  1300 us (77%)
  matrix products  127 us (8%)
  other arithmetic  76.6 us (5%)
  local copies, waits for them, and re-layouts  64.6 us (4%)
  starting transfers between devices  42.8 us (3%)
  blocking collectives  42.5 us (3%)
  between operations  17.6 us (1%)
    ppermute x44, waiting for transfers between devices, from_behind(): return lax.ppermute(block, axis, route)  646 us
    reduce_scatter x1, waiting for transfers between devices, on_device(): lax.psum_scatter(grad_w_mod, 'blk', scatter_dimension=0, tiled=True)  405 us
    reduce_scatter x1, waiting for transfers between devices, on_device(): lax.psum_scatter(grad_w_qkv, 'blk', scatter_dimension=0, tiled=True)  208 us
    ppermute x44, starting transfers between devices, from_behind(): return lax.ppermute(block, axis, route)  42.1 us
    psum x1, blocking collectives, on_device(): full_mods = lax.psum(grad_mods, 'blk')  36.6 us
  transfers between devices with their start and end apart: 50, of which 34 were waited for; matrix products, arithmetic and copies ran while one was open for 10% of the time, Pallas kernels for 0%

commit v1 on v0

v1 whole, which is shorter than its diff:
```python
from functools import partial

import jax
import jax.numpy as jnp
from jax import lax
from jax.experimental import pallas as pl
from jax.experimental.pallas import tpu as pltpu
from jax.sharding import PartitionSpec as P

HEADS = 16
EPS = 1e-06
LANES = 128
SHORT = 16
MESH = pl.DeviceIdType.MESH
BF16 = jnp.bfloat16
F32 = jnp.float32
MIB = 1 << 20


def dot(left, right):
    return jnp.dot(left, right, preferred_element_type=F32)


def dot_rows(left, right):
    return lax.dot_general(left, right, (((1,), (1,)), ((), ())), preferred_element_type=F32)


def dot_frames(left, right):
    return lax.dot_general(left, right, (((0,), (0,)), ((), ())), preferred_element_type=F32)


def normalize(rows):
    mean = jnp.mean(rows, axis=-1, keepdims=True)
    centered = rows - mean
    inverse = lax.rsqrt(jnp.mean(centered * centered, axis=-1, keepdims=True) + EPS)
    return (centered * inverse, inverse)


def norm_back(normed, inverse, grad):
    return inverse * (
        grad
        - jnp.mean(grad, axis=-1, keepdims=True)
        - normed * jnp.mean(grad * normed, axis=-1, keepdims=True)
    )


def whole(shape):
    return pl.BlockSpec(shape, lambda *_: (0,) * len(shape))


def in_hbm():
    return pl.BlockSpec(memory_space=pltpu.HBM)


def rotary_tables(first, frames, seqs, half):
    positions = (first + jnp.arange(frames, dtype=jnp.int32)).astype(F32)
    freqs = 10000.0 ** (-jnp.arange(half, dtype=F32) / half)
    angle = positions[:, None] * freqs[None, :]
    cosines, sines = jnp.cos(angle), jnp.sin(angle)
    reps = LANES // (2 * half)
    cos_table = jnp.tile(jnp.concatenate([cosines, cosines], axis=1), (seqs, reps))
    sin_table = jnp.tile(jnp.concatenate([-sines, sines], axis=1), (seqs, reps))
    return cos_table, sin_table


def rotate(rows, cos_table, sin_table, half):
    lane = lax.broadcasted_iota(jnp.int32, rows.shape, 1)
    partner = jnp.where(
        lax.rem(lane, 2 * half) < half,
        pltpu.roll(rows, LANES - half, 1),
        pltpu.roll(rows, half, 1),
    )
    return rows * cos_table + partner * sin_table


def pre_kernel(sizes, x_ref, time_ref, cos_ref, sin_ref, w_mod, b_mod, w_qkv, b_qkv, mods, hidden, qkv):
    seqs, frames, width, half, mod_steps, span, qkv_span = sizes
    step = pl.program_id(0)

    @pl.when(step < mod_steps)
    def _():
        cols = pl.ds(pl.multiple_of(step * span, span), span)
        mods[:, cols] = dot(time_ref[...], w_mod[...]) + b_mod[...].astype(F32)

    @pl.when(step == mod_steps)
    def _():
        for s in range(seqs):
            normed, _ = normalize(x_ref[s * frames : (s + 1) * frames, :].astype(F32))
            shift, scale = mods[s : s + 1, :width], mods[s : s + 1, width : 2 * width]
            hidden[s * frames : (s + 1) * frames, :] = (normed * (1.0 + scale) + shift).astype(BF16)

    @pl.when(step >= mod_steps)
    def _():
        rows = dot(hidden[...], w_qkv[...]) + b_qkv[...].astype(F32)
        kind = (step - mod_steps) // (width // qkv_span)

        @pl.when(kind < 2)
        def _():
            factor = jnp.where(kind == 0, (2.0 * half) ** (-0.5), 1.0)
            for c in range(qkv_span // LANES):
                part = rows[:, c * LANES : (c + 1) * LANES]
                turned = rotate(part, cos_ref[...], sin_ref[...], half)
                qkv[c] = (turned * factor).astype(BF16)

        @pl.when(kind == 2)
        def _():
            for c in range(qkv_span // LANES):
                qkv[c] = rows[:, c * LANES : (c + 1) * LANES].astype(BF16)


def pre_attention(x, time_act, cos_table, sin_table, w_mod, b_mod, w_qkv, b_qkv, frames):
    tokens, width = x.shape
    seqs = tokens // frames
    half = width // HEADS // 2
    span, qkv_span = 512, 512
    mod_steps = w_mod.shape[1] // span
    per_kind = width // qkv_span
    groups = width // LANES
    sizes = (seqs, frames, width, half, mod_steps, span, qkv_span)

    def at(i):
        return jnp.minimum(i, mod_steps - 1)

    def past(i):
        return jnp.maximum(i - mod_steps, 0)

    return pl.pallas_call(
        partial(pre_kernel, sizes),
        grid=(mod_steps + 3 * per_kind,),
        in_specs=[
            whole((tokens, width)),
            whole((seqs, width)),
            whole((tokens, LANES)),
            whole((tokens, LANES)),
            pl.BlockSpec((width, span), lambda i: (0, at(i))),
            pl.BlockSpec((1, span), lambda i: (0, at(i))),
            pl.BlockSpec((width, qkv_span), lambda i: (0, past(i))),
            pl.BlockSpec((1, qkv_span), lambda i: (0, past(i))),
        ],
        out_specs=[
            whole((seqs, w_mod.shape[1])),
            whole((tokens, width)),
            pl.BlockSpec(
                (qkv_span // LANES, tokens, LANES),
                lambda i: (lax.rem(past(i), per_kind), 0, past(i) // per_kind),
            ),
        ],
        out_shape=[
            jax.ShapeDtypeStruct((seqs, w_mod.shape[1]), F32),
            jax.ShapeDtypeStruct((tokens, width), BF16),
            jax.ShapeDtypeStruct((groups, tokens, 3 * LANES), BF16),
        ],
        compiler_params=pltpu.CompilerParams(vmem_limit_bytes=40 * MIB),
        name="pre_attention",
    )(x, time_act, cos_table, sin_table, w_mod, b_mod[None], w_qkv, b_qkv[None])


class Plan:
    def __init__(self, count, frames, width):
        self.count = count
        self.frames = frames
        self.width = width
        self.groups = min(count, width // LANES)
        self.splits = count // self.groups
        total = count * frames
        short = total // SHORT
        self.total = total
        self.short_rows = min(short, frames)
        self.short_blocks = -(-short // frames)
        self.short = short


def greet_all(count, me, barrier):
    for step in range(1, count):
        pl.semaphore_signal(
            barrier, inc=1, device_id={"blk": lax.rem(me + step, count)}, device_id_type=MESH
        )
    pl.semaphore_wait(barrier, count - 1)


def send(src, dst, send_sem, recv_sem, peer):
    copy = pltpu.make_async_remote_copy(
        src_ref=src, dst_ref=dst, send_sem=send_sem, recv_sem=recv_sem,
        device_id={"blk": peer}, device_id_type=MESH,
    )
    copy.start()
    return copy


def spread_kernel(plan, with_keys, *refs):
    n, g, f = plan.count, plan.groups, plan.frames
    if with_keys:
        rows, q_out, kv_out, short_out, q_send, q_recv, k_send, k_recv, s_send, s_recv = refs
    else:
        rows, q_out, q_send, q_recv = refs
    me = lax.axis_index("blk")
    group, split = lax.rem(me, g), me // g
    greet_all(n, me, pltpu.get_barrier_semaphore())
    waits = []
    if with_keys:
        for step in range(n):
            peer = lax.rem(me + step, n)
            src, dst = rows.at[lax.rem(peer, g), 0:f, LANES : 3 * LANES], kv_out.at[me]
            if step == 0:
                waits.append(pltpu.make_async_copy(src, dst, k_recv.at[0]))
                waits[-1].start()
            else:
                waits.append(send(src, dst, k_send.at[step], k_recv.at[step], peer))
    for step in range(g):
        peer = split * g + lax.rem(group + step, g)
        if with_keys:
            src = rows.at[lax.rem(peer, g), :, 0:LANES]
        else:
            src = rows.at[:, pl.ds(pl.multiple_of(lax.rem(peer, g) * LANES, LANES), LANES)]
        dst = q_out.at[group]
        if step == 0:
            waits.append(pltpu.make_async_copy(src, dst, q_recv.at[0]))
            waits[-1].start()
        else:
            waits.append(send(src, dst, q_send.at[step], q_recv.at[step], peer))
    if with_keys:
        for block in range(plan.short_blocks):
            own = rows.at[group, f : f + plan.short_rows, LANES : 3 * LANES]

            @pl.when(me == block)
            def _():
                copies = []
                for step in range(1, n):
                    peer = lax.rem(me + step, n)
                    src = rows.at[lax.rem(peer, g), f : f + plan.short_rows, LANES : 3 * LANES]
                    copies.append(
                        send(src, short_out.at[block], s_send.at[step], s_recv.at[block], peer)
                    )
                local = pltpu.make_async_copy(own, short_out.at[block], s_recv.at[block])
                local.start()
                for copy in copies:
                    copy.wait_send()

            pltpu.make_async_copy(own, short_out.at[block], s_recv.at[block]).wait()
    for copy in waits:
        copy.wait()


def spread(plan, rows, with_keys, collective_id, name):
    n, g, f = plan.count, plan.groups, plan.frames
    tokens = 2 * f
    outs = [jax.ShapeDtypeStruct((g, tokens, LANES), BF16)]
    sems = [pltpu.SemaphoreType.DMA((g,))] * 2
    if with_keys:
        outs += [
            jax.ShapeDtypeStruct((n, f, 2 * LANES), BF16),
            jax.ShapeDtypeStruct((plan.short_blocks, plan.short_rows, 2 * LANES), BF16),
        ]
        sems += [pltpu.SemaphoreType.DMA((n,))] * 3 + [pltpu.SemaphoreType.DMA((plan.short_blocks,))]
    return pl.pallas_call(
        partial(spread_kernel, plan, with_keys),
        in_specs=[in_hbm()],
        out_specs=[in_hbm()] * len(outs),
        out_shape=outs,
        scratch_shapes=sems,
        compiler_params=pltpu.CompilerParams(collective_id=collective_id, has_side_effects=True),
        name=name,
    )(rows)


def gather_kernel(plan, with_keys, *refs):
    n, g, f = plan.count, plan.groups, plan.frames
    if with_keys:
        q_in, kv_in, short_in, q_out, kv_out, short_out, q_send, q_recv, k_send, k_recv, s_send, s_recv = refs
    else:
        q_in, q_out, q_send, q_recv = refs
    me = lax.axis_index("blk")
    group, split = lax.rem(me, g), me // g
    greet_all(n, me, pltpu.get_barrier_semaphore())
    waits = []
    own_cols = pl.ds(pl.multiple_of(group * LANES, LANES), LANES)
    if with_keys:
        for step in range(n):
            peer = lax.rem(me + step, n)
            for which in range(2):
                src = kv_in.at[which, peer]
                dst = kv_out.at[which, split, :, own_cols]
                if step == 0:
                    waits.append(pltpu.make_async_copy(src, dst, k_recv.at[which, 0]))
                    waits[-1].start()
                else:
                    waits.append(send(src, dst, k_send.at[which, step], k_recv.at[which, step], peer))
    for step in range(g):
        peer = split * g + lax.rem(group + step, g)
        src, dst = q_in.at[lax.rem(peer, g)], q_out.at[:, own_cols]
        if step == 0:
            waits.append(pltpu.make_async_copy(src, dst, q_recv.at[0]))
            waits[-1].start()
        else:
            waits.append(send(src, dst, q_send.at[step], q_recv.at[step], peer))
    if with_keys:
        for block in range(plan.short_blocks):
            dst = short_out.at[:, split, :, own_cols]

            @pl.when(me != block)
            def _():
                send(short_in.at[block], dst, s_send, s_recv.at[me], block).wait_send()

            @pl.when(me == block)
            def _():
                local = pltpu.make_async_copy(short_in.at[block], dst, s_recv.at[block])
                local.start()
                for source in range(n):
                    pltpu.make_async_copy(short_in.at[block], dst, s_recv.at[source]).wait()
    for copy in waits:
        copy.wait()


def gather(plan, parts, with_keys, collective_id, name):
    n, g, f = plan.count, plan.groups, plan.frames
    tokens = 2 * f
    outs = [jax.ShapeDtypeStruct((tokens, plan.width), BF16)]
    sems = [pltpu.SemaphoreType.DMA((g,))] * 2
    if with_keys:
        outs += [
            jax.ShapeDtypeStruct((2, plan.splits, f, plan.width), BF16),
            jax.ShapeDtypeStruct((2, plan.splits, plan.short_rows, plan.width), BF16),
        ]
        sems += [pltpu.SemaphoreType.DMA((2, n))] * 2
        sems += [pltpu.SemaphoreType.DMA(()), pltpu.SemaphoreType.DMA((n,))]
    return pl.pallas_call(
        partial(gather_kernel, plan, with_keys),
        in_specs=[in_hbm()] * len(parts),
        out_specs=[in_hbm()] * len(outs),
        out_shape=outs,
        scratch_shapes=sems,
        compiler_params=pltpu.CompilerParams(collective_id=collective_id, has_side_effects=True),
        name=name,
    )(*parts)


def stacked(rows, head_dim):
    lane = lax.broadcasted_iota(jnp.int32, rows.shape, 1)
    heads = LANES // head_dim
    return jnp.concatenate(
        [jnp.where(lane // head_dim == h, rows, jnp.zeros_like(rows)) for h in range(heads)], axis=0
    )


def unstacked(turned, frames, head_dim):
    heads = LANES // head_dim
    return jnp.concatenate(
        [
            turned[h * head_dim : (h + 1) * head_dim, h * frames : (h + 1) * frames]
            for h in range(heads)
        ],
        axis=0,
    ).T


def attend(queries, keys, values_t, head_dim):
    frames = queries.shape[0]
    scores = dot_rows(keys, stacked(queries, head_dim))
    top = jnp.max(scores, axis=0, keepdims=True)
    weights = jnp.exp(scores - top)
    total = jnp.sum(weights, axis=0, keepdims=True)
    out = dot(values_t, weights.astype(BF16)) / total
    return unstacked(out, frames, head_dim).astype(BF16), top + jnp.log(total)


def attention_kernel(plan, head_dim, q_ref, kv_ref, short_ref, out_ref, lse_ref, long_vt, short_vt):
    f, total, short = plan.frames, plan.total, plan.short

    @pl.when(pl.program_id(0) == 0)
    def _():
        long_vt[...] = kv_ref[:, :, LANES:].reshape(total, LANES).T
        short_vt[...] = short_ref[:, :, LANES:].reshape(short, LANES).T

    long_out, long_lse = attend(
        q_ref[0, :f], kv_ref[:, :, :LANES].reshape(total, LANES), long_vt[...], head_dim
    )
    short_out, short_lse = attend(
        q_ref[0, f:], short_ref[:, :, :LANES].reshape(short, LANES), short_vt[...], head_dim
    )
    out_ref[0, :f] = long_out
    out_ref[0, f:] = short_out
    lse_ref[0, 0:1] = long_lse
    lse_ref[0, 1:2] = short_lse


def attention(plan, head_dim, queries, kv, short_kv):
    g, f = plan.groups, plan.frames
    wide = f * (LANES // head_dim)
    return pl.pallas_call(
        partial(attention_kernel, plan, head_dim),
        grid=(g,),
        in_specs=[
            pl.BlockSpec((1, 2 * f, LANES), lambda i: (i, 0, 0)),
            whole(kv.shape),
            whole(short_kv.shape),
        ],
        out_specs=[
            pl.BlockSpec((1, 2 * f, LANES), lambda i: (i, 0, 0)),
            pl.BlockSpec((1, 2, wide), lambda i: (i, 0, 0)),
        ],
        out_shape=[
            jax.ShapeDtypeStruct((g, 2 * f, LANES), BF16),
            jax.ShapeDtypeStruct((g, 2, wide), F32),
        ],
        scratch_shapes=[
            pltpu.VMEM((LANES, plan.total), BF16),
            pltpu.VMEM((LANES, plan.short), BF16),
        ],
        compiler_params=pltpu.CompilerParams(vmem_limit_bytes=48 * MIB),
        name="attention",
    )(queries, kv, short_kv)


def attend_back(queries, grads, lse, keys, keys_t, values, head_dim):
    frames = queries.shape[0]
    q_heads, g_heads = stacked(queries, head_dim), stacked(grads, head_dim)
    probs = jnp.exp(dot_rows(keys, q_heads) - lse)
    grad_probs = dot_rows(values, g_heads)
    delta = jnp.sum(probs * grad_probs, axis=0, keepdims=True)
    grad_scores = (probs * (grad_probs - delta)).astype(BF16)
    grad_values = dot(probs.astype(BF16), g_heads)
    grad_keys = dot(grad_scores, q_heads)
    grad_queries = unstacked(dot(keys_t, grad_scores), frames, head_dim) * head_dim ** (-0.5)
    return grad_queries.astype(BF16), grad_keys, grad_values


def attention_back_kernel(plan, head_dim, *refs):
    q_ref, g_ref, lse_ref, kv_ref, short_ref, dq_ref, dkv_ref, dshort_ref, long_kt, short_kt, dlong, dsmall = refs
    f, total, short = plan.frames, plan.total, plan.short
    step = pl.program_id(0)

    @pl.when(step == 0)
    def _():
        long_kt[...] = kv_ref[:, :, :LANES].reshape(total, LANES).T
        short_kt[...] = short_ref[:, :, :LANES].reshape(short, LANES).T
        dlong[...] = jnp.zeros_like(dlong)
        dsmall[...] = jnp.zeros_like(dsmall)

    for rows, kv, kt, lse, acc in (
        (slice(0, f), kv_ref, long_kt, lse_ref[0, 0:1], dlong),
        (slice(f, 2 * f), short_ref, short_kt, lse_ref[0, 1:2], dsmall),
    ):
        size = acc.shape[1]
        dq, dk, dv = attend_back(
            q_ref[0, rows],
            g_ref[0, rows],
            lse,
            kv[:, :, :LANES].reshape(size, LANES),
            kt[...],
            kv[:, :, LANES:].reshape(size, LANES),
            head_dim,
        )
        dq_ref[0, rows] = dq
        acc[0] += dk
        acc[1] += dv

    @pl.when(step == pl.num_programs(0) - 1)
    def _():
        dkv_ref[...] = dlong[...].astype(BF16).reshape(dkv_ref.shape)
        for block in range(plan.short_blocks):
            rows = slice(block * plan.short_rows, (block + 1) * plan.short_rows)
            dshort_ref[block] = dsmall[:, rows].astype(BF16)


def attention_back(plan, head_dim, queries, grads, lse, kv, short_kv):
    n, g, f = plan.count, plan.groups, plan.frames
    per_block = pl.BlockSpec((1, 2 * f, LANES), lambda i: (i, 0, 0))
    outs = [
        jax.ShapeDtypeStruct((g, 2 * f, LANES), BF16),
        jax.ShapeDtypeStruct((2, n, f, LANES), BF16),
        jax.ShapeDtypeStruct((plan.short_blocks, 2, plan.short_rows, LANES), BF16),
    ]
    return pl.pallas_call(
        partial(attention_back_kernel, plan, head_dim),
        grid=(g,),
        in_specs=[
            per_block,
            per_block,
            pl.BlockSpec((1,) + lse.shape[1:], lambda i: (i, 0, 0)),
            whole(kv.shape),
            whole(short_kv.shape),
        ],
        out_specs=[per_block, whole(outs[1].shape), whole(outs[2].shape)],
        out_shape=outs,
        scratch_shapes=[
            pltpu.VMEM((LANES, plan.total), BF16),
            pltpu.VMEM((LANES, plan.short), BF16),
            pltpu.VMEM((2, plan.total, LANES), F32),
            pltpu.VMEM((2, plan.short, LANES), F32),
        ],
        compiler_params=pltpu.CompilerParams(vmem_limit_bytes=48 * MIB),
        name="attention_back",
    )(queries, grads, lse, kv, short_kv)


def xy_peers(count, batch):
    b, j = lax.axis_index("batch"), lax.axis_index("blk")
    core, half = lax.rem(b, 2), b // 2
    near, far = lax.rem(j, 2), j // 2
    at_core = (half * 2 + 1 - core, j)
    at_x = ((1 - half) * 2 + core, j)
    at_near = (b, far * 2 + 1 - near)
    return b, j, core, half, near, far, at_core, at_x, at_near


def push(src, dst, sems, index, device):
    copy = pltpu.make_async_remote_copy(
        src_ref=src, dst_ref=dst, send_sem=sems.at[0, index], recv_sem=sems.at[1, index],
        device_id=device, device_id_type=MESH,
    )
    copy.start()
    return copy


def add_into(target, other):
    target[...] = (target[...].astype(F32) + other.astype(F32)).astype(BF16)


def reduce_kernel(count, chunk, parts, out, *scratch):
    rows, columns = parts.shape[1:]
    half_chunk = chunk // 2
    pairs = columns // chunk // 2
    far_count = count // 2
    a_one, a_two, b_one, b_two, far_buf, a1, a2, b1, b2, far_sems, out_x, out_c = scratch
    b, j, core, half, near, far, at_core, at_x, at_near = xy_peers(count, 4)
    barrier = pltpu.get_barrier_semaphore()
    far_peers = [
        (b, lax.rem(far + step, far_count) * 2 + near) for step in range(1, far_count)
    ]
    for device in [at_core, at_x, at_near] + far_peers:
        pl.semaphore_signal(barrier, inc=1, device_id=device, device_id_type=MESH)
    pl.semaphore_wait(barrier, 2 + far_count)

    def cols(base, which):
        return pl.ds(pl.multiple_of(base + which * half_chunk, half_chunk), half_chunk)

    def base_of(k, second):
        return (k + (pairs if second else 0)) * chunk

    parts4 = parts.reshape(far_count, 2, rows, columns)
    stage_one, stage_two, stage_far, stage_x, stage_c = {}, {}, {}, {}, {}

    def start_one(k):
        if k < pairs:
            src = parts.at[:, :, cols(base_of(k, False), 1 - half)]
            stage_one[k, 0] = push(src, a_one.at[k], a1, k, at_x)
            base = base_of(k, True)
            src = parts4.at[:, 1 - near, :, base : base + chunk]
            stage_one[k, 1] = push(src, b_one.at[k], b1, k, at_near)

    def finish_one(k):
        stage_one[k, 0].wait()
        add_into(a_one.at[k], parts[:, :, cols(base_of(k, False), half)])
        src = a_one.at[k].reshape(far_count, 2, rows, half_chunk).at[:, 1 - near]
        stage_two[k, 0] = push(src, a_two.at[k], a2, k, at_near)
        stage_one[k, 1].wait()
        base = base_of(k, True)
        add_into(b_one.at[k], parts4[:, near, :, base : base + chunk])
        src = b_one.at[k, :, :, cols(0, 1 - half)]
        stage_two[k, 1] = push(src, b_two.at[k], b2, k, at_x)

    def finish_two(k):
        stage_two[k, 0].wait()
        add_into(a_two.at[k], a_one.at[k].reshape(far_count, 2, rows, half_chunk)[:, near])
        stage_two[k, 1].wait()
        add_into(b_two.at[k], b_one[k, :, :, cols(0, half)])
        for which, buf in enumerate((a_two, b_two)):
            for step in range(1, far_count):
                peer = lax.rem(far + step, far_count)
                stage_far[k, which, step] = push(
                    buf.at[k, peer],
                    far_buf.at[which, k, step - 1],
                    far_sems,
                    (which * pairs + k) * far_count + step,
                    (b, peer * 2 + near),
                )

    def finish_far(k):
        for which, buf in enumerate((a_two, b_two)):
            total = buf[k, far].astype(F32)
            for step in range(1, far_count):
                stage_far[k, which, step].wait()
                total = total + far_buf[which, k, step - 1].astype(F32)
            own = cols(base_of(k, which), half)
            out[core, :, own] = total.astype(BF16)
            place = out.at[core, :, own]
            stage_x[k, which] = push(place, place, out_x, which * pairs + k, at_x)
            stage_c[k, which, 0] = push(place, place, out_c, (which * pairs + k) * 2, at_core)

    def finish_x(k):
        for which in range(2):
            stage_x[k, which].wait()
            place = out.at[core, :, cols(base_of(k, which), 1 - half)]
            stage_c[k, which, 1] = push(place, place, out_c, (which * pairs + k) * 2 + 1, at_core)

    start_one(0)
    start_one(1)
    for t in range(pairs + 3):
        if t < pairs:
            finish_one(t)
            start_one(t + 2)
        if 0 <= t - 1 < pairs:
            finish_two(t - 1)
        if 0 <= t - 2 < pairs:
            finish_far(t - 2)
        if 0 <= t - 3 < pairs:
            finish_x(t - 3)
    for copy in stage_c.values():
        copy.wait()


def reduce_weights(parts, chunk, collective_id):
    count, rows, columns = parts.shape
    half_chunk, pairs, far_count = chunk // 2, columns // chunk // 2, count // 2

    def sems(size):
        return pltpu.SemaphoreType.DMA((2, size))

    vmem = pl.BlockSpec(memory_space=pltpu.VMEM)
    return pl.pallas_call(
        partial(reduce_kernel, count, chunk),
        in_specs=[vmem],
        out_specs=vmem,
        out_shape=jax.ShapeDtypeStruct((2, rows, columns), BF16),
        scratch_shapes=[
            pltpu.VMEM((pairs, count, rows, half_chunk), BF16),
            pltpu.VMEM((pairs, far_count, rows, half_chunk), BF16),
            pltpu.VMEM((pairs, far_count, rows, chunk), BF16),
            pltpu.VMEM((pairs, far_count, rows, half_chunk), BF16),
            pltpu.VMEM((2, pairs, far_count - 1, rows, half_chunk), BF16),
            sems(pairs),
            sems(pairs),
            sems(pairs),
            sems(pairs),
            sems(2 * pairs * far_count),
            sems(2 * pairs),
            sems(4 * pairs),
        ],
        compiler_params=pltpu.CompilerParams(
            collective_id=collective_id, has_side_effects=True, vmem_limit_bytes=56 * MIB
        ),
        name="reduce_weights",
    )(parts)


def small_kernel(count, batch, parts, out, arrived, mine, first, second, third):
    b, j = lax.axis_index("batch"), lax.axis_index("blk")
    barrier = pltpu.get_barrier_semaphore()
    along = [(b, lax.rem(j + step, count)) for step in range(1, count)]
    across = [(lax.rem(b + step, batch), j) for step in range(1, batch)]
    for device in along + across:
        pl.semaphore_signal(barrier, inc=1, device_id=device, device_id_type=MESH)
    pl.semaphore_wait(barrier, count + batch - 2)
    copies = []
    for step, device in enumerate(along):
        copies.append(push(parts.at[device[1]], arrived.at[step], first, step, device))
    total = parts[j]
    for step in range(count - 1):
        copies[step].wait()
        total = total + arrived[step]
    mine[...] = total
    out[b, j] = total
    copies = []
    for step, device in enumerate(along):
        copies.append(push(mine, out.at[b, j], second, step, device))
    for copy in copies:
        copy.wait()
    copies = []
    for step, device in enumerate(across):
        copies.append(push(out.at[b], out.at[b], third, step, device))
    for copy in copies:
        copy.wait()


def small_sums(parts, batch, collective_id):
    count = parts.shape[0]
    vmem = pl.BlockSpec(memory_space=pltpu.VMEM)
    return pl.pallas_call(
        partial(small_kernel, count, batch),
        in_specs=[vmem],
        out_specs=vmem,
        out_shape=jax.ShapeDtypeStruct((batch,) + parts.shape, F32),
        scratch_shapes=[
            pltpu.VMEM((count - 1,) + parts.shape[1:], F32),
            pltpu.VMEM(parts.shape[1:], F32),
            pltpu.SemaphoreType.DMA((2, count - 1)),
            pltpu.SemaphoreType.DMA((2, count - 1)),
            pltpu.SemaphoreType.DMA((2, batch - 1)),
        ],
        compiler_params=pltpu.CompilerParams(collective_id=collective_id, has_side_effects=True),
        name="small_sums",
    )(parts)


def core_swap(array, batch):
    return lax.ppermute(array, "batch", [(i, i ^ 1) for i in range(batch)])


def half_columns(array, which):
    size = array.shape[1] // 2
    return lax.dynamic_slice_in_dim(array, which * size, size, axis=1)


def weight_part(left, right, core, batch):
    other_left = core_swap(left, batch)
    other_right = core_swap(half_columns(right, 1 - core), batch)
    both_left = jnp.concatenate([left, other_left], axis=0)
    both_right = jnp.concatenate([half_columns(right, core), other_right], axis=0)
    return dot_frames(both_left, both_right).astype(BF16)


def on_device(
    inputs,
    time_embed,
    lengths,
    cotangent,
    w_mod,
    b_mod,
    w_qkv,
    b_qkv,
    w_out,
    b_out,
    w_up,
    b_up,
    w_down,
    b_down,
):
    seqs, frames, width = inputs.shape
    tokens = seqs * frames
    head_dim = width // HEADS
    count, batch = lax.axis_size("blk"), lax.axis_size("batch")
    me = lax.axis_index("blk")
    core = lax.rem(lax.axis_index("batch"), 2)
    plan = Plan(count, frames, width)
    swap = lengths[0] < lengths[1]

    def ordered(array):
        return jnp.where(swap, array[::-1], array)

    embed = ordered(time_embed).astype(F32)
    time_silu, silu_pull = jax.vjp(jax.nn.silu, embed)
    time_act = time_silu.astype(BF16)
    cos_table, sin_table = rotary_tables(me * frames, frames, seqs, head_dim // 2)
    x = ordered(inputs).reshape(tokens, width)
    mods, hidden_a, qkv = pre_attention(
        x, time_act, cos_table, sin_table, w_mod, b_mod, w_qkv, b_qkv, frames
    )
    queries, kv, short_kv = spread(plan, qkv, True, 0, "spread_qkv")
    attn_groups, lse = attention(plan, head_dim, queries, kv, short_kv)
    (attn_low,) = gather(plan, (attn_groups,), False, 1, "gather_attention")

    def per_frame(piece):
        return jnp.repeat(piece, frames, axis=0)

    def per_seq(rows):
        return jnp.sum(rows.reshape(seqs, frames, -1), axis=1)

    shift_a, scale_a, gate_a, shift_f, scale_f, gate_f = [
        per_frame(piece) for piece in jnp.split(mods, 6, axis=-1)
    ]
    residual = x.astype(F32)
    branch_a = dot(attn_low, w_out) + b_out.astype(F32)
    mixed = residual + gate_a * branch_a
    norm_f, inverse_f = normalize(mixed)
    hidden_f = (norm_f * (1.0 + scale_f) + shift_f).astype(BF16)
    pre_act = dot(hidden_f, w_up) + b_up.astype(F32)
    act_f32, gelu_pull = jax.vjp(partial(jax.nn.gelu, approximate=True), pre_act)
    act_low = act_f32.astype(BF16)
    branch_f = dot(act_low, w_down) + b_down.astype(F32)
    output = mixed + gate_f * branch_f
    grad_out = ordered(cotangent).reshape(tokens, width).astype(F32)
    grad_gate_f = per_seq(grad_out * branch_f)
    grad_ff = (gate_f * grad_out).astype(BF16)
    part_down = weight_part(act_low, grad_ff, core, batch)
    grad_pre = gelu_pull(dot_rows(grad_ff, w_down))[0].astype(BF16)
    part_up = weight_part(hidden_f, grad_pre, core, batch)
    grad_hidden_f = dot_rows(grad_pre, w_up)
    grad_scale_f = per_seq(grad_hidden_f * norm_f)
    grad_shift_f = per_seq(grad_hidden_f)
    grad_mixed = grad_out + norm_back(norm_f, inverse_f, grad_hidden_f * (1.0 + scale_f))
    grad_gate_a = per_seq(grad_mixed * branch_a)
    grad_branch_a = (gate_a * grad_mixed).astype(BF16)
    part_out = weight_part(attn_low, grad_branch_a, core, batch)
    grad_attn = dot_rows(grad_branch_a, w_out).astype(BF16)

    (grads,) = spread(plan, grad_attn, False, 2, "spread_grad")
    dq, dkv, dshort = attention_back(plan, head_dim, queries, grads, lse, kv, short_kv)
    dq, dkv, dshort = gather(plan, (dq, dkv, dshort), True, 3, "gather_grads")
    dkv = jnp.sum(dkv.astype(F32), axis=1)
    dshort = jnp.where(me < plan.short_blocks, jnp.sum(dshort.astype(F32), axis=1), 0.0)
    dshort = jnp.pad(dshort, ((0, 0), (0, frames - plan.short_rows), (0, 0)))
    grad_kv = jnp.concatenate([dkv, dshort], axis=1)

    def turned_back(rows):
        groups = rows.reshape(tokens, -1, 2, head_dim // 2)
        cosines = cos_table[:, None, : head_dim // 2]
        sines = sin_table[:, None, head_dim // 2 : head_dim]
        first, second = groups[:, :, 0], groups[:, :, 1]
        return jnp.stack(
            [first * cosines + second * sines, second * cosines - first * sines], axis=2
        ).reshape(tokens, width)

    grad_qkv = jnp.concatenate(
        [turned_back(dq.astype(F32)), turned_back(grad_kv[0]), grad_kv[1]], axis=1
    ).astype(BF16)
    part_qkv = weight_part(hidden_a, grad_qkv, core, batch)
    grad_hidden_a = dot_rows(grad_qkv, w_qkv)
    norm_a, inverse_a = normalize(residual)
    grad_scale_a = per_seq(grad_hidden_a * norm_a)
    grad_shift_a = per_seq(grad_hidden_a)
    grad_inputs = grad_mixed + norm_back(norm_a, inverse_a, grad_hidden_a * (1.0 + scale_a))
    grad_mods = jnp.concatenate(
        [grad_shift_a, grad_scale_a, grad_gate_a, grad_shift_f, grad_scale_f, grad_gate_f], axis=-1
    )
    biases = [jnp.sum(g.astype(F32), axis=0) for g in (grad_qkv, grad_branch_a, grad_pre, grad_ff)]

    mod_cols = mods.shape[1] // count
    bias_sizes = [bias.shape[0] // count for bias in biases]
    own = (jnp.arange(count) == me)[:, None]
    pieces = [
        grad_mods.reshape(seqs, count, mod_cols).transpose(1, 0, 2).reshape(count, -1),
        *[bias.reshape(count, -1) for bias in biases],
        jnp.where(
            own,
            time_act.astype(F32).reshape(seqs, count, -1).transpose(1, 0, 2).reshape(count, -1),
            0.0,
        ),
    ]
    flat = jnp.concatenate(pieces, axis=1)
    size = flat.shape[1]
    flat = jnp.pad(flat, ((0, 0), (0, -size % (8 * LANES))))
    sums = small_sums(flat.reshape(count, -1, LANES), batch, 4).reshape(batch, count, -1)
    mods_all = sums[:, :, : seqs * mod_cols].reshape(batch, count, seqs, mod_cols)
    mods_all = mods_all.transpose(0, 2, 1, 3).reshape(batch * seqs, -1)
    mine = lax.dynamic_index_in_dim(sums, me, axis=1, keepdims=False)
    grad_b_mod = jnp.sum(mine[:, : seqs * mod_cols].reshape(batch * seqs, mod_cols), axis=0)
    offset = seqs * mod_cols
    bias_total = jnp.sum(mine, axis=0)
    grad_biases = []
    for bias_size in bias_sizes:
        grad_biases.append(bias_total[offset : offset + bias_size])
        offset += bias_size
    times = mine[:, offset : offset + seqs * (width // count)].reshape(batch * seqs, -1)
    grad_w_mod = dot_frames(times.astype(BF16), mods_all.astype(BF16))
    own_mods = lax.dynamic_slice_in_dim(mods_all, lax.axis_index("batch") * seqs, seqs, axis=0)
    grad_silu = dot_rows(own_mods.astype(BF16), w_mod)
    grad_time = ordered(silu_pull(grad_silu)[0])

    rows = width // count
    split_down = part_down.reshape(count, -1, rows, width // 2)
    split_down = [split_down[:, i] for i in range(split_down.shape[1])]
    parts = jnp.concatenate(
        [p.reshape(count, rows, -1) for p in (part_qkv, part_out, part_up)] + split_down, axis=2
    )
    totals = reduce_weights(parts, 512, 5).astype(F32)
    ends = [3 * width // 2, 2 * width, 3 * width]
    grad_w_qkv, grad_w_out, grad_w_up, down = [
        jnp.concatenate([piece[0], piece[1]], axis=1) for piece in jnp.split(totals, ends, axis=2)
    ]
    down = down.reshape(rows, 2, -1, width // 2).transpose(2, 0, 1, 3)
    grad_w_down = down.reshape(-1, width)
    return (
        ordered(output.reshape(seqs, frames, width)),
        ordered(grad_inputs.reshape(seqs, frames, width)),
        grad_time,
        grad_w_mod,
        grad_b_mod,
        grad_w_qkv,
        grad_biases[0],
        grad_w_out,
        grad_biases[1],
        grad_w_up,
        grad_biases[2],
        grad_w_down,
        grad_biases[3],
    )


def solution(mesh):
    frame_spec, weight_spec = P("batch", "blk", None), P("blk", None)
    return jax.shard_map(
        on_device,
        mesh=mesh,
        in_specs=(frame_spec, P("batch", None), P("batch"), frame_spec) + (P(),) * 10,
        out_specs=(frame_spec, frame_spec, P("batch", None)) + (weight_spec, P("blk")) * 5,
        check_vma=False,
    )
```

time: 1690 us -> 365 us (0.22)
  waiting for transfers between devices: 1300 us -> 0.02 us
  Pallas kernels: 0 us -> 244 us
  matrix products: 127 us -> 42.6 us
  other arithmetic: 76.6 us -> 19.3 us
  blocking collectives: 42.5 us -> 0 us
  starting transfers between devices: 42.8 us -> 2.57 us
    ppermute x44 -> x8, waiting for transfers between devices: 646 us -> 0.02 us  [core_swap(): return lax.ppermute(array, 'batch', [(i, i ^ 1) for i in range(batch)])]
    reduce_scatter x5 -> x0, waiting for transfers between devices: 643 us -> none  [the longest x1 405 us: on_device(): lax.psum_scatter(grad_w_mod, 'blk', scatter_dimension=0, tiled=True)]
    pallas_call x0 -> x9, Pallas kernels: none -> 244 us  [the longest x1 98.5 us: reduce_weights(): pl.pallas_call(partial(reduce_kernel, count, chunk), in_specs=[vmem], out...]
    dot_general x70 -> x13, matrix products: 127 us -> 42.6 us  [the longest x5 17.8 us: dot_rows(): lax.dot_general(left, right, (((1,), (1,)), ((), ())), preferred_element_...]
    psum x2 -> x0, blocking collectives: 42.5 us -> none  [the longest x1 36.6 us: on_device(): full_mods = lax.psum(grad_mods, 'blk')]
    ppermute x44 -> x8, starting transfers between devices: 42.1 us -> 2.57 us  [core_swap(): return lax.ppermute(array, 'batch', [(i, i ^ 1) for i in range(batch)])]
    add x37 -> x1, other arithmetic: 30.7 us -> 0.01 us  [on_device(): 1.0 + scale_a]
    while x92 -> x0, local copies, waits for them, and re-layouts: 30.6 us -> none
  transfers between devices with their start and end apart: 50 -> 8, of which waited for: 34 -> 0; matrix products, arithmetic and copies ran while one was open for 10% -> 19% of each run, Pallas kernels for 0% -> 21%
where the time goes in v1:
time: 365 us; the launch traced here: 361 us
  Pallas kernels  244 us (67%)
  local copies, waits for them, and re-layouts  49.7 us (14%)
  matrix products  42.6 us (12%)
  other arithmetic  19.3 us (5%)
    pallas_call x1, Pallas kernels, reduce_weights(): pl.pallas_call(partial(reduce_kernel, count, chunk), in_specs=[vmem], out...  98.5 us
    pallas_call x2, Pallas kernels, gather(): pl.pallas_call(partial(gather_kernel, plan, with_keys), in_specs=[in_hbm(...  47.7 us
    pallas_call x2, Pallas kernels, spread(): pl.pallas_call(partial(spread_kernel, plan, with_keys), in_specs=[in_hbm(...  44.4 us
    unnamed x125, local copies, waits for them, and re-layouts  25.2 us
    pallas_call x1, Pallas kernels, small_sums(): pl.pallas_call(partial(small_kernel, count, batch), in_specs=[vmem], out_...  18.4 us
    dot_general x5, matrix products, dot_rows(): lax.dot_general(left, right, (((1,), (1,)), ((), ())), preferred_element_...  17.8 us
    pallas_call x1, Pallas kernels, pre_attention(): pl.pallas_call(partial(pre_kernel, sizes), grid=(mod_steps + 3 * per_kind...  15 us
    dot_general x3, matrix products, dot(): return jnp.dot(left, right, preferred_element_type=F32)  12.5 us
  transfers between devices with their start and end apart: 8, of which 0 were waited for; matrix products, arithmetic and copies ran while one was open for 19% of the time, Pallas kernels for 21%

profile of v1, /device:TPU:0, one launch (start us, length us, event | category | flops | bytes accessed | tf_op | source)
XLA Modules:
  0.0 360.9 jit_solution(13515579723964891607)
XLA Ops:
  0.7 1.4 fusion.76
  2.1 2.7 rev.19
  6.1 1.4 convert_reduce_fusion.2
  8.2 2.8 copy-done.2
  11.0 15.0 %pre_attention.1 = (f32[2,6144]{1,0:T(2,128)S(1)}, bf16[256,1024]{1,0:T(8,128)(2,1)S(1)}, bf16[8,256,384]{2,1,0:T(8,128)(2,1)S(1)}) custom-call(bf16[256,1024]{1,0:T(8,128)(2,1)S(1)} %bitcast.195, bf16[2,1024]{1,0:T(2,128)(2,1)S(1)} %get-tuple-element.54.time_ref, f32[256,128]{1,0:T(8,128)S(1)} %copy.29.cos_ref, f32[256,128]{1,0:T(8,128)S(1)} %copy.30.sin_ref, ...), custom_call_target="tpu_custom_call" | custom-call | tf_op jit(solution)/shard_map/pre_attention/pallas_call | solution.py:127
  26.0 1.1 copy-done.8
  27.9 28.3 %spread_qkv.1 = (bf16[8,256,128]{2,1,0:T(8,128)(2,1)}, bf16[8,128,256]{2,1,0:T(8,128)(2,1)}, bf16[1,64,256]{2,1,0:T(8,128)(2,1)}) custom-call(bf16[8,256,384]{2,1,0:T(8,128)(2,1)} %copy-done.8), custom_call_target="tpu_custom_call" | custom-call | tf_op jit(solution)/shard_map/spread_qkv/pallas_call | solution.py:255
  59.1 8.8 %attention.1 = (bf16[8,256,128]{2,1,0:T(8,128)(2,1)S(1)}, f32[8,2,256]{2,1,0:T(2,128)S(1)}) custom-call(bf16[8,256,128]{2,1,0:T(8,128)(2,1)S(1)} %copy-done.3, bf16[8,128,256]{2,1,0:T(8,128)(2,1)S(1)} %copy-done.5, bf16[1,64,256]{2,1,0:T(8,128)(2,1)S(1)} %copy-done.12), custom_call_target="tpu_custom_call" | custom-call | tf_op jit(solution)/shard_map/attention/pallas_call | solution.py:389
  68.7 15.6 %gather_attention.1 = bf16[256,1024]{1,0:T(8,128)(2,1)} custom-call(bf16[8,256,128]{2,1,0:T(8,128)(2,1)} %copy-done.11), custom_call_target="tpu_custom_call" | custom-call | tf_op jit(solution)/shard_map/gather_attention/pallas_call | solution.py:326
  84.4 2.9 fusion.72
  89.5 1.3 fusion.77
  90.8 1.1 copy-done.27
  91.8 4.8 %convert_reduce_fusion.1 = (f32[2048]{0:T(1024)S(1)}, bf16[256,2048]{1,0:T(8,128)(2,1)S(1)}, bf16[256,2048]{1,0:T(8,128)(2,1)}) fusion(f32[256,2048]{1,0:T(8,128)S(1)} %fusion.77, f32[2048]{0:T(1024)S(1)} %convert_element_type.117, bf16[256,1024]{1,0:T(8,128)(2,1)} %fusion.27, bf16[1024,2048]{1,0:T(8,128)(2,1)S(1)} %copy-done.27), kind=kOutput, calls=%fused_computation.18 | convolution fusion | flops 1086846976 | bytes 8929280 | tf_op jit(solution)/shard_map/dot_general | solution.py:21
  96.6 1.5 fusion.44
  98.2 4.8 %convert_reduce_fusion.4 = (f32[1024]{0:T(1024)S(1)}, bf16[256,1024]{1,0:T(8,128)(2,1)S(1)}, f32[256,1024]{1,0:T(8,128)}, f32[256,1024]{1,0:T(8,128)}, f32[256,1024]{1,0:T(8,128)}) fusion(f32[2,1024]{1,0:T(2,128)S(1)} %get-tuple-element.96, f32[256]{0:T(256)S(1)} %broadcast_multiply_fusion.3, f32[256,1024]{1,0:T(8,128)S(1)} %get-tuple-element.65, ...), kind=kOutput, calls=%fused_computation.88 | convolution fusion | flops 1078197248 | bytes 11571201 | tf_op jit(solution)/shard_map/dot_general | solution.py:21
  103.8 1.6 convolution_convert_fusion.4.refs_0_
  105.4 16.2 %spread_grad.1.refs_1_ = bf16[8,256,128]{2,1,0:T(8,128)(2,1)} custom-call(bf16[256,1024]{1,0:T(8,128)(2,1)} %convolution_convert_fusion.4.refs_0_), custom_call_target="tpu_custom_call" | custom-call | tf_op jit(solution)/shard_map/spread_grad/pallas_call | solution.py:255
  123.7 10.7 %attention_back.1 = (bf16[8,256,128]{2,1,0:T(8,128)(2,1)S(1)}, bf16[2,8,128,128]{3,2,1,0:T(8,128)(2,1)S(1)}, bf16[1,2,64,128]{3,2,1,0:T(8,128)(2,1)S(1)}) custom-call(bf16[8,256,128]{2,1,0:T(8,128)(2,1)S(1)} %copy-done.4, bf16[8,256,128]{2,1,0:T(8,128)(2,1)S(1)} %copy-done.7, f32[8,2,256]{2,1,0:T(2,128)S(1)} %get-tuple-element.33.refs_2_, ...), custom_call_target="tpu_custom_call" | custom-call | tf_op jit(solution)/shard_map/attention_back/pallas_call | solution.py:473
  136.5 32.1 %gather_grads.1 = (bf16[256,1024]{1,0:T(8,128)(2,1)}, bf16[2,1,128,1024]{3,2,1,0:T(8,128)(2,1)}, bf16[2,1,64,1024]{3,2,1,0:T(8,128)(2,1)}) custom-call(bf16[8,256,128]{2,1,0:T(8,128)(2,1)} %copy-done.9, bf16[2,8,128,128]{3,2,1,0:T(8,128)(2,1)} %copy-done.10, bf16[1,2,64,128]{3,2,1,0:T(8,128)(2,1)} %copy-done.14), custom_call_target="tpu_custom_call" | custom-call | tf_op jit(solution)/shard_map/gather_grads/pallas_call | solution.py:326
  168.7 1.1 bitcast_convert_fusion
  171.2 1.1 slice.124
  172.2 1.2 copy.31
  173.5 1.6 copy.33
  178.1 1.3 convert_reduce_fusion
  179.4 1.1 copy-done.19
  180.6 1.3 constant_dynamic-slice_fusion.7
  183.1 2.1 constant_dynamic-slice_fusion.3
  185.8 5.3 %fusion.43 = (f32[256]{0:T(256)S(1)}, f32[256]{0:T(256)S(1)}, f32[256,1024]{1,0:T(8,128)S(1)}) fusion(f32[2,1024]{1,0:T(2,128)S(1)} %get-tuple-element.92, f32[256]{0:T(256)S(1)} %rsqrt_bitcast_fusion, f32[256]{0:T(256)S(1)} %get-tuple-element.99, bf16[2,128,1024]{2,1,0:T(8,128)(2,1)S(1)} %get-tuple-element.63, bf16[256,3072]{1,0:T(8,128)(2,1)} %copy-done.19, ...), kind=kOutput, calls=%fused_computation.92 | convolution fusion | flops 1612447232 | bytes 9449472 | tf_op jit(solution)/shard_map/dot_general | solution.py:25
  192.4 1.5 fusion.74
  195.1 18.4 %small_sums.1 = f32[4,8,24,128]{3,2,1,0:T(8,128)} custom-call(f32[8,24,128]{2,1,0:T(8,128)} %bitcast.218), custom_call_target="tpu_custom_call" | custom-call | tf_op jit(solution)/shard_map/small_sums/pallas_call | solution.py:678
  214.7 8.1 %fusion.59 = f32[2,1024]{1,0:T(2,128)S(1)} fusion(bf16[1024,6144]{1,0:T(8,128)(2,1)} %w_mod.1, bf16[8,6144]{1,0:T(8,128)(2,1)S(1)} %bitcast.220, s32[]{:T(128)S(6)} %select_n.89, bf16[2,1024]{1,0:T(2,128)(2,1)S(1)} %rev.19, bf16[2,1024]{1,0:T(2,128)(2,1)S(1)} %copy-done.45, pred[]{:T(512)} %bitcast), kind=kOutput, calls=%fused_computation.155 | convolution fusion | flops 25188352 | bytes 12623877 | tf_op jit(solution)/shard_map/dot_general | solution.py:25
  223.3 1.6 reverse_select_fusion
  225.0 2.3 fusion.78
  231.2 1.9 convolution_convert_fusion.3
  233.6 2.7 convolution_convert_fusion.2
  236.3 3.0 convolution_convert_fusion
  239.3 2.0 constant_dynamic-update-slice_fusion.14
  241.3 1.1 constant_dynamic-update-slice_fusion.13
  242.4 1.6 constant_dynamic-update-slice_fusion.12
  244.0 2.5 convolution_convert_fusion.1
  246.5 1.1 fusion.29
  247.6 1.1 fusion.28.parts
  248.8 98.5 %reduce_weights.1 = bf16[2,128,4096]{2,1,0:T(8,128)(2,1)} custom-call(bf16[8,128,4096]{2,1,0:T(8,128)(2,1)} %fusion.28.parts), custom_call_target="tpu_custom_call" | custom-call | tf_op jit(solution)/shard_map/reduce_weights/pallas_call | solution.py:620
  347.3 2.1 convert_element_type.142
  353.1 1.5 concatenate.82
  356.3 1.2 copy.49
  357.5 1.3 pad_maximum_fusion.1
  359.6 1.1 pad_maximum_fusion.2
  (202 shorter events, 33.2 us)
Async XLA Ops:
  0.6 83.8 %copy-start = (bf16[1024,1024]{1,0:T(8,128)(2,1)S(1)}, bf16[1024,1024]{1,0:T(8,128)(2,1)}, u32[]{:S(2)}) copy-start(bf16[1024,1024]{1,0:T(8,128)(2,1)} %param.22) | copy-start | bytes 6291460
  0.7 7.4 %copy-start.46 = (bf16[6144]{0:T(1024)(128)(2,1)S(1)}, bf16[6144]{0:T(1024)(128)(2,1)}, u32[]{:S(2)}) copy-start(bf16[6144]{0:T(1024)(128)(2,1)} %param.19) | copy-start | bytes 36868
  0.7 7.5 %copy-start.47 = (bf16[3072]{0:T(1024)(128)(2,1)S(1)}, bf16[3072]{0:T(1024)(128)(2,1)}, u32[]{:S(2)}) copy-start(bf16[3072]{0:T(1024)(128)(2,1)} %param.21) | copy-start | bytes 18436
  8.2 2.8 copy-start.2
  26.0 1.1 copy-start.8
  27.9 56.5 %copy-start.49 = (bf16[1024]{0:T(1024)(128)(2,1)S(1)}, bf16[1024]{0:T(1024)(128)(2,1)}, u32[]{:S(2)}) copy-start(bf16[1024]{0:T(1024)(128)(2,1)} %param.23) | copy-start | bytes 6148
  84.3 146.8 %collective-permute-start.2 = (bf16[256,1024]{1,0:T(8,128)(2,1)}, bf16[256,1024]{1,0:T(8,128)(2,1)}, u32[]{:S(2)}, u32[]{:S(2)}) collective-permute-start(bf16[256,1024]{1,0:T(8,128)(2,1)} %gather_attention.1), channel_id=1, source_target_pairs={{0,8},{8,0},{16,24},{24,16},{1,9},{9,1},{17,25},{25,17},{2,10},{10... | collective-permute-start | bytes 1572872 | tf_op jit(solution)/shard_map/ppermute | solution.py:696
  84.4 5.0 %copy-start.29 = (bf16[2048,1024]{1,0:T(8,128)(2,1)S(1)}, bf16[2048,1024]{1,0:T(8,128)(2,1)}, u32[]{:S(2)}) copy-start(bf16[2048,1024]{1,0:T(8,128)(2,1)} %param.26) | copy-start | bytes 12582916
  87.4 10.8 %copy-start.17 = (f32[256,1024]{1,0:T(8,128)}, f32[256,1024]{1,0:T(8,128)S(1)}, u32[]{:S(2)}) copy-start(f32[256,1024]{1,0:T(8,128)S(1)} %get-tuple-element.65) | copy-start | bytes 3145732
  87.4 1.8 copy-start.48
  87.4 1.8 copy-start.23
  88.7 144.3 %collective-permute-start.4 = (bf16[256,1024]{1,0:T(8,128)(2,1)}, bf16[256,1024]{1,0:T(8,128)(2,1)}, u32[]{:S(2)}, u32[]{:S(2)}) collective-permute-start(bf16[256,1024]{1,0:T(8,128)(2,1)} %fusion.27), channel_id=1, source_target_pairs={{0,8},{8,0},{16,24},{24,16},{1,9},{9,1},{17,25},{25,17},{2,10},{10... | collective-permute-start | bytes 1572872 | tf_op jit(solution)/shard_map/ppermute | solution.py:696
  89.4 1.3 copy-start.35
  89.4 2.4 copy-start.27
  96.6 1.5 copy-start.28
  96.6 1.5 copy-start.50
  98.1 4.8 %copy-start.21 = (f32[256,1024]{1,0:T(8,128)}, f32[256,1024]{1,0:T(8,128)S(1)}, u32[]{:S(2)}) copy-start(f32[256,1024]{1,0:T(8,128)S(1)} %get-tuple-element.107) | copy-start | bytes 3145732
  103.8 17.8 %copy-start.4 = (bf16[8,256,128]{2,1,0:T(8,128)(2,1)S(1)}, bf16[8,256,128]{2,1,0:T(8,128)(2,1)}, u32[]{:S(2)}) copy-start(bf16[8,256,128]{2,1,0:T(8,128)(2,1)} %get-tuple-element.29.q_ref.refs_0_) | copy-start | bytes 1572868
  103.8 17.8 %copy-start.13 = (bf16[1,64,256]{2,1,0:T(8,128)(2,1)S(1)}, bf16[1,64,256]{2,1,0:T(8,128)(2,1)}, u32[]{:S(2)}) copy-start(bf16[1,64,256]{2,1,0:T(8,128)(2,1)} %get-tuple-element.31.short_ref.refs_4_) | copy-start | bytes 98308
  121.6 1.0 copy-start.6
  179.4 1.1 copy-start.19
  179.4 2.4 copy-start.40
  181.8 3.4 copy-start.18
  181.8 3.4 copy-start.22
  181.8 54.5 %collective-permute-start.1 = (bf16[256,1536]{1,0:T(8,128)(2,1)}, bf16[256,1536]{1,0:T(8,128)(2,1)}, u32[]{:S(2)}, u32[]{:S(2)}) collective-permute-start(bf16[256,1536]{1,0:T(8,128)(2,1)} %get-tuple-element.76), channel_id=1, source_target_pairs={{0,8},{8,0},{16,24},{24,16},{1,9},{9,1},{17,25},{25,17},{2,10},{10... | collective-permute-start | bytes 2359304 | tf_op jit(solution)/shard_map/ppermute | solution.py:696
  182.6 47.1 %collective-permute-start.3 = (bf16[256,512]{1,0:T(8,128)(2,1)}, bf16[256,512]{1,0:T(8,128)(2,1)}, u32[]{:S(2)}, u32[]{:S(2)}) collective-permute-start(bf16[256,512]{1,0:T(8,128)(2,1)} %get-tuple-element.89), channel_id=1, source_target_pairs={{0,8},{8,0},{16,24},{24,16},{1,9},{9,1},{17,25},{25,17},{2,10},{10... | collective-permute-start | bytes 786440 | tf_op jit(solution)/shard_map/ppermute | solution.py:696
  185.2 48.4 %collective-permute-start.5 = (bf16[256,1024]{1,0:T(8,128)(2,1)}, bf16[256,1024]{1,0:T(8,128)(2,1)}, u32[]{:S(2)}, u32[]{:S(2)}) collective-permute-start(bf16[256,1024]{1,0:T(8,128)(2,1)} %get-tuple-element.82), channel_id=1, source_target_pairs={{0,8},{8,0},{16,24},{24,16},{1,9},{9,1},{17,25},{25,17},{2,10},{10... | collective-permute-start | bytes 1572872 | tf_op jit(solution)/shard_map/ppermute | solution.py:696
  185.8 5.7 %copy-start.31 = (f32[256,1024]{1,0:T(8,128)S(1)}, f32[256,1024]{1,0:T(8,128)}, u32[]{:S(2)}) copy-start(f32[256,1024]{1,0:T(8,128)} %get-tuple-element.59) | copy-start | bytes 3145732
  191.2 1.2 copy-start.25
  192.4 1.6 copy-start.24
  192.4 1.6 copy-start.32
  193.9 20.7 %copy-start.45 = (bf16[2,1024]{1,0:T(2,128)(2,1)S(1)}, bf16[2,1024]{1,0:T(2,128)(2,1)}, u32[]{:S(2)}) copy-start(bf16[2,1024]{1,0:T(2,128)(2,1)} %param.15) | copy-start | bytes 12292
  214.6 8.7 %copy-start.26 = (f32[256,1024]{1,0:T(8,128)S(1)}, f32[256,1024]{1,0:T(8,128)}, u32[]{:S(2)}) copy-start(f32[256,1024]{1,0:T(8,128)} %get-tuple-element.84) | copy-start | bytes 3145732
  214.7 8.7 %copy-start.30 = (f32[256,1024]{1,0:T(8,128)S(1)}, f32[256,1024]{1,0:T(8,128)}, u32[]{:S(2)}) copy-start(f32[256,1024]{1,0:T(8,128)} %get-tuple-element.85) | copy-start | bytes 3145732
  225.0 4.6 %copy-start.36 = (bf16[256,1024]{1,0:T(8,128)(2,1)S(1)}, bf16[256,1024]{1,0:T(8,128)(2,1)}, u32[]{:S(2)}) copy-start(bf16[256,1024]{1,0:T(8,128)(2,1)} %copy-done.35) | copy-start | bytes 1572868
  225.0 4.7 %copy-start.16 = (bf16[256,1024]{1,0:T(8,128)(2,1)S(1)}, bf16[256,1024]{1,0:T(8,128)(2,1)}, u32[]{:S(2)}) copy-start(bf16[256,1024]{1,0:T(8,128)(2,1)} %copy-done.15) | copy-start | bytes 1572868
  225.0 6.2 %copy-start.34 = (bf16[256,1024]{1,0:T(8,128)(2,1)S(1)}, bf16[256,1024]{1,0:T(8,128)(2,1)}, u32[]{:S(2)}) copy-start(bf16[256,1024]{1,0:T(8,128)(2,1)} %gather_attention.1) | copy-start | bytes 1572868
  229.7 6.6 %collective-permute-start = (bf16[256,1024]{1,0:T(8,128)(2,1)S(1)}, bf16[256,1024]{1,0:T(8,128)(2,1)S(1)}, u32[]{:S(2)}, u32[]{:S(2)}) collective-permute-start(bf16[256,1024]{1,0:T(8,128)(2,1)S(1)} %copy-done.16), channel_id=1, source_target_pairs={{0,8},{8,0},{16,24},{24,16},{1,9},{9,1},{17,25},{25,17},{2,10},{10... | collective-permute-start | bytes 1572872 | tf_op jit(solution)/shard_map/ppermute | solution.py:696
  231.1 12.8 %collective-permute-start.6 = (bf16[256,2048]{1,0:T(8,128)(2,1)}, bf16[256,2048]{1,0:T(8,128)(2,1)S(1)}, u32[]{:S(2)}, u32[]{:S(2)}) collective-permute-start(bf16[256,2048]{1,0:T(8,128)(2,1)} %get-tuple-element.74), channel_id=1, source_target_pairs={{0,8},{8,0},{16,24},{24,16},{1,9},{9,1},{17,25},{25,17},{2,10},{10... | collective-permute-start | bytes 3145736 | tf_op jit(solution)/shard_map/ppermute | solution.py:696
  233.0 10.9 %collective-permute-start.7 = (bf16[256,512]{1,0:T(8,128)(2,1)S(1)}, bf16[256,512]{1,0:T(8,128)(2,1)S(1)}, u32[]{:S(2)}, u32[]{:S(2)}) collective-permute-start(bf16[256,512]{1,0:T(8,128)(2,1)S(1)} %get-tuple-element.87), channel_id=1, source_target_pairs={{0,8},{8,0},{16,24},{24,16},{1,9},{9,1},{17,25},{25,17},{2,10},{10... | collective-permute-start | bytes 786440 | tf_op jit(solution)/shard_map/ppermute | solution.py:696
  233.6 2.7 copy-start.44
  350.3 1.9 copy-start.20
  355.5 2.0 copy-start.33
  357.5 1.3 copy-start.42
  357.5 1.3 copy-start.43
  357.5 2.1 copy-start.37
  357.5 2.1 copy-start.38
  357.5 3.2 copy-start.1
  (11 other events, 9.5 us)
